TPU v7x, 768 devices: a whole 4x8x12 slice. The times are simulated.
768 devices in a mesh: tm: 48 (over y, z_hi, core), stripe: 16 (over z_lo, x).
Axes of the slice: x: 4, y: 8, z: 12 (z_hi: 3, z_lo: 4; z = z_hi * 4 + z_lo), core: 2. Of those that a mesh axis runs over, the one named last changes fastest.
Arguments:
- tokens: bfloat16 [96, 768, 1024], P('tm', 'stripe'), may hold values from -17 to 17, as said below
- time_input: bfloat16 [1024, 1536], replicated, may hold values from -0.1875 to 0.1875
- time_output: bfloat16 [512, 1024], replicated, may hold values from -0.25 to 0.25
- space_input: bfloat16 [1024, 1536], replicated, may hold values from -0.1875 to 0.1875
- space_output: bfloat16 [512, 1024], replicated, may hold values from -0.25 to 0.25
Outputs:
- encoded: bfloat16 [96, 768, 1024], P('tm', 'stripe')
Inputs may be any that keep to these rules, and one draw needn't show every extreme that they name: Real-valued embeddings whose features and tokens have different scales.
All inputs are finite; a program needn't handle non-finite values.
Results may differ from a plain program's by a relative error of at most 0.01.
Values may be sent and summed in bfloat16 or wider, within the bound.
No kernel may reach another device: no remote copies, remote signals or barrier semaphores. Data moves between devices by JAX's collectives and lax.ppermute only.
A program may use at most 64 MiB of HBM per device.

v0:
```python
import math

import jax
import jax.numpy as jnp
from jax import lax
from jax.sharding import PartitionSpec as P

HEAD_DIM = 64


def layer_norm(values):
    wide = values.astype(jnp.float32)
    centre = jnp.mean(wide, axis=-1, keepdims=True)
    spread = jnp.mean((wide - centre) ** 2, axis=-1, keepdims=True)
    return ((wide - centre) * lax.rsqrt(spread + 1e-05)).astype(jnp.bfloat16)


def normalize(proj):
    query = proj[..., 0, :]
    key_part = proj[..., 1, :]
    query = query * lax.rsqrt(jnp.mean(query * query, axis=-1, keepdims=True) + 1e-06)
    key_part = key_part * lax.rsqrt(jnp.mean(key_part * key_part, axis=-1, keepdims=True) + 1e-06)
    return jnp.stack([query, key_part, proj[..., 2, :]], axis=-2).astype(jnp.bfloat16)


def attend_middle(query, key_part, value):
    scale = 2.0 / math.sqrt(HEAD_DIM)
    scores = jnp.einsum("qic,kic->iqk", query, key_part, preferred_element_type=jnp.float32) * scale
    weights = jnp.exp(scores)
    total = jnp.sum(weights, axis=-1)
    summed = jnp.einsum(
        "iqk,kic->qic", weights.astype(jnp.bfloat16), value, preferred_element_type=jnp.float32
    )
    return (summed / jnp.transpose(total)[:, :, None]).astype(jnp.bfloat16)


def per_device(tokens, time_input, time_output, space_input, space_output):
    frames, patches, width = tokens.shape
    inner = time_output.shape[0]
    heads = inner // HEAD_DIM
    time_count = lax.axis_size("tm")
    owned = patches * heads // time_count
    proj = jnp.dot(
        layer_norm(tokens).reshape(frames * patches, width),
        time_input,
        preferred_element_type=jnp.float32,
    )
    packed = normalize(proj.reshape(frames, patches, heads, 3, HEAD_DIM))
    flat = packed.reshape(frames, patches * heads * 3 * HEAD_DIM)
    moved = lax.all_to_all(flat, "tm", split_axis=1, concat_axis=0, tiled=True)
    moved = moved.reshape(frames * time_count, owned, 3, HEAD_DIM)
    attn_time = attend_middle(moved[:, :, 0, :], moved[:, :, 1, :], moved[:, :, 2, :])
    returned = lax.all_to_all(
        attn_time.reshape(frames * time_count, owned * HEAD_DIM),
        "tm",
        split_axis=0,
        concat_axis=1,
        tiled=True,
    )
    mixed = tokens.astype(jnp.float32).reshape(frames * patches, width) + jnp.dot(
        returned.reshape(frames * patches, inner), time_output, preferred_element_type=jnp.float32
    )
    hidden = mixed.astype(jnp.bfloat16).reshape(frames, patches, width)
    normed = layer_norm(hidden)
    proj_space = jnp.dot(
        normed.reshape(frames * patches, width), space_input, preferred_element_type=jnp.float32
    )
    packed_space = normalize(proj_space.reshape(frames, patches, heads, 3, HEAD_DIM))
    query = packed_space[:, :, :, 0, :]
    pairs = packed_space[:, :, :, 1:, :].reshape(frames, patches, heads * 2 * HEAD_DIM)
    scale = 2.0 / math.sqrt(HEAD_DIM)
    piece = lax.all_gather(pairs, "stripe", axis=1, tiled=True)
    count = piece.shape[1]
    piece = piece.reshape(frames, count, heads, 2, HEAD_DIM)
    scores = (
        jnp.einsum(
            "fqhc,fkhc->fhqk", query, piece[:, :, :, 0, :], preferred_element_type=jnp.float32
        )
        * scale
    )
    weights = jnp.exp(scores)
    total = jnp.sum(weights, axis=-1)
    summed = jnp.einsum(
        "fhqk,fkhc->fqhc",
        weights.astype(jnp.bfloat16),
        piece[:, :, :, 1, :],
        preferred_element_type=jnp.float32,
    )
    summed, total = (summed, total)
    attn_space = (summed / jnp.transpose(total, (0, 2, 1))[:, :, :, None]).astype(jnp.bfloat16)
    branch = jnp.dot(
        attn_space.reshape(frames * patches, inner),
        space_output,
        preferred_element_type=jnp.float32,
    )
    final = hidden.astype(jnp.float32).reshape(frames * patches, width) + branch
    return final.astype(jnp.bfloat16).reshape(frames, patches, width)


def solution(mesh):
    placed = (P("tm", "stripe", None), P(), P(), P(), P())
    return jax.shard_map(
        per_device, mesh=mesh, in_specs=placed, out_specs=P("tm", "stripe", None), check_vma=False
    )
```

profile of v0, /device:TPU:8, one launch (start us, length us, event | category | flops | bytes accessed | tf_op | source)
XLA Modules:
  0.0 186.3 jit_solution(15992585345779532448)
XLA Ops:
  6.5 0.0 copy-start
  6.5 1.1 convert_reduce_fusion
  7.7 1.1 multiply_reduce_fusion.5
  8.8 0.0 copy-start.2
  8.8 4.7 %copy.24 = bf16[1024,1536]{0,1:T(8,128)(2,1)} copy(bf16[1024,1536]{1,0:T(8,128)(2,1)} %param.6) | data formatting | bytes 6291456 | tf_op args[1]
  13.5 0.0 copy-done.2
  13.5 3.6 %fusion.18 = f32[2,48,8,3,64]{4,1,3,2,0:T(8,128)S(1)} fusion(bf16[8,3,64,1024,1]{3,2,1,0,4:T(8,128)(2,1)} %bitcast.90, bf16[2,48,1024]{2,1,0:T(8,128)(2,1)S(1)} %copy-done.2, f32[2,48]{1,0:T(2,128)S(1)} %add_rsqrt_fusion.4, f32[2,48]{1,0:T(2,128)S(1)} %broadcast_multiply_fusion), kind=kOutput, calls=%fused_computation.39 | convolution fusion | flops 302383104 | bytes 3932928 | tf_op jit(solution)/shard_map/dot_general | solution.py:43
  17.1 0.3 multiply_reduce_fusion.4
  17.4 0.3 multiply_convert_fusion.4
  17.7 0.1 pad_maximum_fusion
  17.8 0.4 copy.42
  18.3 0.5 reshape.131
  18.8 34.1 %all_to_all.29 = bf16[2,48,1536]{2,0,1:T(2,128)(2,1)S(1)} all-to-all(bf16[2,48,1536]{2,0,1:T(2,128)(2,1)S(1)} %reshape.131), channel_id=1, replica_groups=mesh['tm'=48,'stripe'=16] {'tm'}, dimensions={1} | all-to-all | bytes 589824 | tf_op jit(solution)/shard_map/all_to_all | solution.py:50
  52.9 0.4 reshape.121
  53.3 0.8 fusion.30
  54.2 0.4 copy.44
  54.5 0.4 copy.45
  54.9 0.4 copy.46
  55.3 0.3 fusion.31
  55.6 0.2 fusion.16
  55.8 0.2 copy.31
  55.9 0.8 all_to_all.24
  56.7 9.8 %all-to-all-start.1 = ((bf16[48,2,512]{2,1,0:T(2,128)(2,1)}), bf16[48,2,512]{2,1,0:T(2,128)(2,1)S(1)}, u32[]{:S(2)}, u32[]{:S(2)}) async-start(bf16[48,2,512]{2,1,0:T(2,128)(2,1)} %all_to_all.24), calls=%async_computation.1 | async-start | bytes 196608 | tf_op jit(solution)/shard_map/all_to_all | solution.py:53
  66.6 0.0 all-gather.2.cloned.1.call-start
  66.6 4.6 %copy.33 = bf16[1024,1536]{0,1:T(8,128)(2,1)} copy(bf16[1024,1536]{1,0:T(8,128)(2,1)} %param.8) | data formatting | bytes 6291456 | tf_op args[3]
  71.3 6.8 %all-to-all-done.1 = bf16[48,2,512]{2,1,0:T(2,128)(2,1)S(1)} async-done(((bf16[48,2,512]{2,1,0:T(2,128)(2,1)}), bf16[48,2,512]{2,1,0:T(2,128)(2,1)S(1)}, u32[]{:S(2)}, u32[]{:S(2)}) %all-to-all-start.1) | async-done | bytes 98336 | tf_op jit(solution)/shard_map/all_to_all | solution.py:53
  78.1 0.0 copy-done
  78.1 0.4 fusion.32
  78.5 0.2 multiply_reduce_fusion.2
  78.7 0.1 multiply_convert_fusion.2
  78.8 3.5 %fusion.33 = f32[2,48,8,3,64]{4,1,3,2,0:T(8,128)S(1)} fusion(bf16[2,48,1024,1,1]{2,1,4,3,0:T(8,128)(2,1)S(1)} %bitcast.95, bf16[8,3,64,1024,1]{3,2,1,0,4:T(8,128)(2,1)} %bitcast.89), kind=kOutput, calls=%fused_computation.60 | convolution fusion | flops 301989888 | bytes 3932160 | tf_op jit(solution)/shard_map/dot_general | solution.py:65
  82.4 0.3 multiply_reduce_fusion
  82.7 0.2 multiply_convert_fusion.1
  82.9 0.1 pad_maximum_fusion.1
  83.0 0.3 copy.34
  83.3 1.0 reshape.123
  84.2 0.0 all-gather.2.cloned.1.call-update
  84.3 85.9 %all-gather.2.cloned.1.call-done = bf16[2,768,1024]{2,1,0:T(8,128)(2,1)} async-done(((bf16[2,48,1024]{2,1,0:T(8,128)(2,1)}), bf16[2,768,1024]{2,1,0:T(8,128)(2,1)}) %all-gather.2.cloned.1.call-update) | async-done | bytes 3145744 | tf_op jit(solution)/shard_map/all_gather | solution.py:72
  170.2 4.7 %copy.35 = bf16[2,768,1024]{1,2,0:T(8,128)(2,1)} copy(bf16[2,768,1024]{2,1,0:T(8,128)(2,1)} %all-gather.2.cloned.1.call-done) | data formatting | bytes 6291456 | tf_op jit(solution)/shard_map/all_gather | solution.py:72
  174.8 0.0 copy-start.1
  174.8 2.2 %fusion = (f32[2,8,48]{2,1,0:T(8,128)S(1)}, f32[2,8,48,768]{3,2,1,0:T(8,128)S(1)}) fusion(bf16[2,768,8,2,64]{1,4,3,2,0:T(8,128)(2,1)} %bitcast.91, f32[2,48,8,3,64]{4,1,3,2,0:T(8,128)S(1)} %fusion.33, f32[2,48,8]{1,2,0:T(8,128)S(1)} %add_rsqrt_fusion), kind=kOutput, calls=%fused_computation.1 | convolution fusion | flops 76774656 | bytes 4336640 | tf_op jit(solution)/shard_map/fqhc,fkhc->fhqk/dot_general | solution.py:76
  177.0 0.2 copy-done.1
  177.2 0.0 copy-start.3
  177.2 0.6 fusion.9
  177.8 0.1 copy.38
  177.9 0.2 reshape.125
  178.0 0.4 copy-done.3
  178.4 1.0 fusion.14
  (10 shorter events, 0.1 us)
Async XLA Ops:
  6.5 71.5 %copy-start = (bf16[512,1024]{1,0:T(8,128)(2,1)S(1)}, bf16[512,1024]{1,0:T(8,128)(2,1)}, u32[]{:S(2)}) copy-start(bf16[512,1024]{1,0:T(8,128)(2,1)} %param.7) | copy-start | bytes 3145732
  8.8 4.7 %copy-start.2 = (bf16[2,48,1024]{2,1,0:T(8,128)(2,1)S(1)}, bf16[2,48,1024]{2,1,0:T(8,128)(2,1)}, u32[]{:S(2)}) copy-start(bf16[2,48,1024]{2,1,0:T(8,128)(2,1)} %param.5) | copy-start | bytes 589828
  56.7 21.3 %all-to-all-start.1 = ((bf16[48,2,512]{2,1,0:T(2,128)(2,1)}), bf16[48,2,512]{2,1,0:T(2,128)(2,1)S(1)}, u32[]{:S(2)}, u32[]{:S(2)}) async-start(bf16[48,2,512]{2,1,0:T(2,128)(2,1)} %all_to_all.24), calls=%async_computation.1 | async-start | bytes 196608 | tf_op jit(solution)/shard_map/all_to_all | solution.py:53
  66.6 103.6 %all-gather.2.cloned.1.call-start = ((), (), s32[]{:S(2)}) async-start(), calls=%async_computation.2 | async-start | bytes 3342336 | tf_op jit(solution)/shard_map/all_gather | solution.py:72
  174.8 2.4 %copy-start.1 = (bf16[2,768,1024]{1,2,0:T(8,128)(2,1)S(1)}, bf16[2,768,1024]{1,2,0:T(8,128)(2,1)}, u32[]{:S(2)}) copy-start(bf16[2,768,1024]{1,2,0:T(8,128)(2,1)} %copy.35) | copy-start | bytes 9437188
  177.2 1.2 copy-start.3
Sparse Core Ops, SparseCore 0:
  84.4 85.7 all-gather.1
where the time goes:
time: 187 us; the launch traced here: 186 us
  waiting for transfers between devices  92.7 us (50%)
  blocking collectives  34.1 us (18%)
  local copies, waits for them, and re-layouts  20.4 us (11%)
  between operations  13.6 us (7%)
  matrix products  11.8 us (6%)
  starting transfers between devices  9.88 us (5%)
  other arithmetic  3.84 us (2%)
    all_gather x1, waiting for transfers between devices, per_device(): piece = lax.all_gather(pairs, 'stripe', axis=1, tiled=True)  85.9 us
    all_to_all x1, blocking collectives, per_device(): moved = lax.all_to_all(flat, 'tm', split_axis=1, concat_axis=0, tiled=True)  34.1 us
    unnamed x13, local copies, waits for them, and re-layouts  11 us
    all_to_all x1, starting transfers between devices, per_device(): lax.all_to_all(attn_time.reshape(frames * time_count, owned * HEAD_DIM),...  9.83 us
    all_to_all x1, waiting for transfers between devices, per_device(): lax.all_to_all(attn_time.reshape(frames * time_count, owned * HEAD_DIM),...  6.77 us
    all_gather x1, local copies, waits for them, and re-layouts, per_device(): piece = lax.all_gather(pairs, 'stripe', axis=1, tiled=True)  4.69 us
  transfers between devices with their start and end apart: 2, of which 2 were waited for; matrix products, arithmetic and copies ran while one was open for 2% of the time, Pallas kernels for 0%

commit v1 on v0

v1 whole, which is shorter than its diff:
```python
import math

import jax
import jax.numpy as jnp
from jax import lax
from jax.sharding import PartitionSpec as P

HEAD_DIM = 64


def layer_norm(values):
    wide = values.astype(jnp.float32)
    centre = jnp.mean(wide, axis=-1, keepdims=True)
    spread = jnp.mean((wide - centre) ** 2, axis=-1, keepdims=True)
    return ((wide - centre) * lax.rsqrt(spread + 1e-05)).astype(jnp.bfloat16)


def normalize(proj):
    query = proj[..., 0, :]
    key_part = proj[..., 1, :]
    query = query * lax.rsqrt(jnp.mean(query * query, axis=-1, keepdims=True) + 1e-06)
    key_part = key_part * lax.rsqrt(jnp.mean(key_part * key_part, axis=-1, keepdims=True) + 1e-06)
    return (
        query.astype(jnp.bfloat16),
        key_part.astype(jnp.bfloat16),
        proj[..., 2, :].astype(jnp.bfloat16),
    )


def per_device(tokens, time_input, time_output, space_input, space_output):
    frames, patches, width = tokens.shape
    inner = time_output.shape[0]
    heads = inner // HEAD_DIM
    time_count = lax.axis_size("tm")
    stripe_count = lax.axis_size("stripe")
    scale = 2.0 / math.sqrt(HEAD_DIM)
    span = frames * time_count
    moved = lax.all_to_all(tokens, "tm", split_axis=1, concat_axis=0, tiled=True)
    moved = moved.reshape(span, width)
    proj = jnp.dot(layer_norm(moved), time_input, preferred_element_type=jnp.float32)
    query, key_part, value = normalize(proj.reshape(span, heads, 3, HEAD_DIM))
    scores = jnp.einsum("qhc,khc->hqk", query, key_part, preferred_element_type=jnp.float32)
    weights = jnp.exp(scores * scale)
    total = jnp.sum(weights, axis=-1)
    summed = jnp.einsum(
        "hqk,khc->qhc", weights.astype(jnp.bfloat16), value, preferred_element_type=jnp.float32
    )
    attn_time = (summed / jnp.transpose(total)[:, :, None]).astype(jnp.bfloat16)
    returned = lax.all_to_all(
        attn_time.reshape(span, 1, inner), "tm", split_axis=0, concat_axis=1, tiled=True
    )
    mixed = tokens.astype(jnp.float32).reshape(frames * patches, width) + jnp.dot(
        returned.reshape(frames * patches, inner), time_output, preferred_element_type=jnp.float32
    )
    hidden = mixed.astype(jnp.bfloat16)
    proj_space = jnp.dot(layer_norm(hidden), space_input, preferred_element_type=jnp.float32)
    packed = jnp.stack(
        normalize(proj_space.reshape(frames, patches, heads, 3, HEAD_DIM)), axis=3
    )
    packed = jnp.transpose(packed, (0, 2, 1, 3, 4)).reshape(
        frames * heads, patches, 3 * HEAD_DIM
    )
    pair = lax.all_to_all(packed, "stripe", split_axis=0, concat_axis=0, tiled=True)
    pair = pair.reshape(stripe_count * patches, 3 * HEAD_DIM)
    scores = jnp.dot(
        pair[:, :HEAD_DIM], pair[:, HEAD_DIM : 2 * HEAD_DIM].T, preferred_element_type=jnp.float32
    )
    weights = jnp.exp(scores * scale)
    total = jnp.sum(weights, axis=-1, keepdims=True)
    summed = jnp.dot(
        weights.astype(jnp.bfloat16), pair[:, 2 * HEAD_DIM :], preferred_element_type=jnp.float32
    )
    attn_space = (summed / total).astype(jnp.bfloat16)
    back = lax.all_to_all(
        attn_space.reshape(stripe_count, patches, HEAD_DIM),
        "stripe",
        split_axis=0,
        concat_axis=0,
        tiled=True,
    )
    back = jnp.transpose(back.reshape(frames, heads, patches, HEAD_DIM), (0, 2, 1, 3))
    branch = jnp.dot(
        back.reshape(frames * patches, inner), space_output, preferred_element_type=jnp.float32
    )
    final = hidden.astype(jnp.float32) + branch
    return final.astype(jnp.bfloat16).reshape(frames, patches, width)


def solution(mesh):
    placed = (P("tm", "stripe", None), P(), P(), P(), P())
    return jax.shard_map(
        per_device, mesh=mesh, in_specs=placed, out_specs=P("tm", "stripe", None), check_vma=False
    )
```

time: 187 us -> 137 us (0.73)
  waiting for transfers between devices: 92.7 us -> 8.52 us
  blocking collectives: 34.1 us -> 54.2 us
  between operations: 13.6 us -> 0.16 us
  other arithmetic: 3.84 us -> 14.8 us
  starting transfers between devices: 9.88 us -> 20 us
  local copies, waits for them, and re-layouts: 20.4 us -> 28.2 us
    all_gather x1 -> x0, waiting for transfers between devices: 85.9 us -> none  [per_device(): piece = lax.all_gather(pairs, 'stripe', axis=1, tiled=True)]
    all_to_all x1 -> x3, blocking collectives: 34.1 us -> 54.2 us  [the longest x1 20.9 us: per_device(): lax.all_to_all(packed, 'stripe', split_axis=0, concat_axis=0, tiled=True)]
    all_to_all x1, starting transfers between devices: 9.83 us -> 20 us  [per_device(): lax.all_to_all(tokens, 'tm', split_axis=1, concat_axis=0, tiled=True)]
    reshape x3 -> x6, local copies, waits for them, and re-layouts: 1.58 us -> 10.7 us  [the longest x1 2.77 us: per_device(): proj_space.reshape(frames, patches, heads, 3, HEAD_DIM)]
    reduce_sum x2, other arithmetic: 0.57 us -> 5.85 us  [normalize(): jnp.mean(query * query, axis=-1, keepdims=True) + 1e-06]
    all_gather x1 -> x0, local copies, waits for them, and re-layouts: 4.69 us -> none  [per_device(): piece = lax.all_gather(pairs, 'stripe', axis=1, tiled=True)]
    convert_element_type x0 -> x1, other arithmetic: none -> 3.89 us  [normalize(): query.astype(jnp.bfloat16)]
    transpose x0 -> x1, other arithmetic: none -> 2.62 us  [per_device(): jnp.transpose(packed, (0, 2, 1, 3, 4))]
  transfers between devices with their start and end apart: 2 -> 1, of which waited for: 2 -> 1; matrix products, arithmetic and copies ran while one was open for 2% -> 3% of each run, Pallas kernels for 0% -> 0%
where the time goes in v1:
time: 137 us; the launch traced here: 136 us
  blocking collectives  54.2 us (40%)
  local copies, waits for them, and re-layouts  28.2 us (21%)
  starting transfers between devices  20 us (15%)
  other arithmetic  14.8 us (11%)
  matrix products  10.4 us (8%)
  waiting for transfers between devices  8.52 us (6%)
    all_to_all x1, blocking collectives, per_device(): lax.all_to_all(packed, 'stripe', split_axis=0, concat_axis=0, tiled=True)  20.9 us
    all_to_all x1, blocking collectives, per_device(): lax.all_to_all(attn_time.reshape(span, 1, inner), 'tm', split_axis=0, con...  20.5 us
    all_to_all x1, starting transfers between devices, per_device(): lax.all_to_all(tokens, 'tm', split_axis=1, concat_axis=0, tiled=True)  20 us
    all_to_all x1, blocking collectives, per_device(): lax.all_to_all(attn_space.reshape(stripe_count, patches, HEAD_DIM), 'stri...  12.8 us
    unnamed x9, local copies, waits for them, and re-layouts  10.3 us
    all_to_all x1, waiting for transfers between devices, per_device(): lax.all_to_all(tokens, 'tm', split_axis=1, concat_axis=0, tiled=True)  8.52 us
    reduce_sum x2, other arithmetic, normalize(): jnp.mean(query * query, axis=-1, keepdims=True) + 1e-06  5.85 us
    convert_element_type x1, other arithmetic, normalize(): query.astype(jnp.bfloat16)  3.89 us
  transfers between devices with their start and end apart: 1, of which 1 were waited for; matrix products, arithmetic and copies ran while one was open for 3% of the time, Pallas kernels for 0%

profile of v1, /device:TPU:8, one launch (start us, length us, event | category | flops | bytes accessed | tf_op | source)
XLA Modules:
  0.0 136.3 jit_solution(15114305445587854519)
XLA Ops:
  0.0 0.0 copy-start
  0.0 2.0 %copy.33 = bf16[2,48,1024]{2,0,1:T(2,128)(2,1)} copy(bf16[2,48,1024]{2,1,0:T(8,128)(2,1)} %param.5) | data formatting | bytes 393216 | tf_op args[0]
  2.0 20.0 %all-to-all-start = ((bf16[2,48,1024]{2,0,1:T(2,128)(2,1)}), bf16[2,48,1024]{2,0,1:T(2,128)(2,1)S(1)}, u32[]{:S(2)}, u32[]{:S(2)}) async-start(bf16[2,48,1024]{2,0,1:T(2,128)(2,1)} %copy.33), calls=%async_computation | async-start | bytes 393216 | tf_op jit(solution)/shard_map/all_to_all | solution.py:38
  22.0 4.6 %copy.34 = bf16[1024,1536]{0,1:T(8,128)(2,1)} copy(bf16[1024,1536]{1,0:T(8,128)(2,1)} %param.6) | data formatting | bytes 6291456 | tf_op args[1]
  26.6 8.5 %all-to-all-done = bf16[2,48,1024]{2,0,1:T(2,128)(2,1)S(1)} async-done(((bf16[2,48,1024]{2,0,1:T(2,128)(2,1)}), bf16[2,48,1024]{2,0,1:T(2,128)(2,1)S(1)}, u32[]{:S(2)}, u32[]{:S(2)}) %all-to-all-start) | async-done | bytes 196640 | tf_op jit(solution)/shard_map/all_to_all | solution.py:38
  35.1 0.2 fusion.18
  35.4 0.4 fusion.21
  35.8 0.3 fusion.22
  36.1 0.1 reshape.143
  36.1 2.9 %fusion.28 = f32[96,8,3,64]{0,3,2,1:T(8,128)S(1)} fusion(bf16[8,3,64,1024]{3,2,1,0:T(8,128)(2,1)} %bitcast.78, bf16[96,1024,1,1]{1,0,2,3:T(8,128)(2,1)S(1)} %reshape.143), kind=kOutput, calls=%fused_computation.44 | convolution fusion | flops 301989888 | bytes 3932160 | tf_op jit(solution)/shard_map/dot_general | solution.py:40
  39.0 0.1 multiply_reduce_fusion.4
  39.1 0.3 fusion.38
  39.4 0.2 fusion.10
  39.6 0.5 broadcast.136
  40.1 0.7 reduce.5
  40.8 0.1 copy.52
  41.0 20.5 %all_to_all.34 = bf16[48,2,512]{2,1,0:T(2,128)(2,1)S(1)} all-to-all(bf16[48,2,512]{2,1,0:T(2,128)(2,1)S(1)} %reshape.146), channel_id=1, replica_groups=mesh['tm'=48,'stripe'=16] {'tm'}, dimensions={0} | all-to-all | bytes 196608 | tf_op jit(solution)/shard_map/all_to_all | solution.py:49
  61.5 0.1 reshape.147
  61.6 0.6 reduce.4
  62.2 1.7 %fusion.39 = (f32[96]{0:T(128)S(1)}, f32[96,1024]{1,0:T(8,128)S(1)}) fusion(bf16[96,512]{1,0:T(8,128)(2,1)S(1)} %bitcast.85, bf16[512,1024]{1,0:T(8,128)(2,1)} %param.7, bf16[96,1024]{1,0:T(8,128)(2,1)} %bitcast.81), kind=kOutput, calls=%fused_computation.63 | convolution fusion | flops 101154720 | bytes 1737088 | tf_op jit(solution)/shard_map/dot_general | solution.py:52
  63.9 0.2 multiply_reduce_fusion.2
  64.1 0.0 copy-done
  64.1 1.5 %fusion.23 = f32[96,1536]{1,0:T(8,128)} fusion(bf16[1024,1536]{1,0:T(8,128)(2,1)S(1)} %copy-done, f32[96,1024]{1,0:T(8,128)S(1)} %get-tuple-element.14, f32[96]{0:T(128)S(1)} %add_rsqrt_fusion.5, f32[96]{0:T(128)S(1)} %broadcast_multiply_fusion.1), kind=kOutput, calls=%fused_computation.39 | convolution fusion | flops 302284800 | bytes 4129536 | tf_op jit(solution)/shard_map/dot_general | solution.py:56
  65.6 2.8 %reshape.133 = f32[2,48,8,3,64]{4,3,2,1,0:T(4,128)} reshape(f32[96,1536]{1,0:T(8,128)} %fusion.23) | data formatting | bytes 1179648 | tf_op jit(solution)/shard_map/reshape | solution.py:58
  68.4 5.8 %multiply_reduce_fusion.1 = (f32[2,48,8]{2,1,0:T(8,128)}, f32[2,48,8]{2,1,0:T(8,128)}) fusion(f32[2,48,8,3,64]{4,3,2,1,0:T(4,128)} %reshape.133), kind=kLoop, calls=%fused_computation.29 | loop fusion | flops 195072 | bytes 399360 | tf_op jit(solution)/shard_map/reduce_sum | solution.py:21
  74.2 2.6 %slice.74 = bf16[2,48,8,1,64]{4,3,2,1,0:T(2,128)(2,1)} slice(f32[2,48,8,3,64]{4,3,2,1,0:T(4,128)} %reshape.133), slice={[0:2], [0:48], [0:8], [2:3], [0:64]} | slice | bytes 196608 | tf_op jit(solution)/shard_map/slice | solution.py:26
  76.7 0.9 copy.38
  77.6 0.7 copy.39
  78.3 0.9 copy.40
  79.2 0.7 copy.41
  79.9 3.9 %multiply_convert_fusion.1 = (bf16[2,48,8,1,64]{4,3,2,1,0:T(2,128)(2,1)S(1)}, bf16[2,48,8,1,64]{4,3,2,1,0:T(2,128)(2,1)S(1)}) fusion(f32[2,48,8,3,64]{4,3,2,1,0:T(4,128)} %reshape.133, f32[2,48,8]{2,1,0:T(8,128)} %copy.39, f32[2,48,8]{2,1,0:T(8,128)} %copy.41), kind=kLoop, calls=%fused_computation.28 | loop fusion | flops 196608 | bytes 595968 | tf_op jit(solution)/shard_map/convert_element_type | solution.py:24
  83.8 2.6 %maximum_bitcast_fusion = bf16[2,8,48,3,64]{4,3,1,2,0:T(4,128)(2,1)S(1)} fusion(bf16[2,48,8,1,64]{4,3,2,1,0:T(2,128)(2,1)} %slice.74, bf16[2,48,8,1,64]{4,3,2,1,0:T(2,128)(2,1)S(1)} %get-tuple-element.10, bf16[2,48,8,1,64]{4,3,2,1,0:T(2,128)(2,1)S(1)} %get-tuple-element.9), kind=kLoop, calls=%fused_computation.17 | loop fusion | flops 884736 | bytes 589824 | tf_op jit(solution)/shard_map/transpose | solution.py:60
  86.4 1.3 copy.42
  87.7 2.3 %reshape.134 = bf16[16,48,192]{2,1,0:T(8,128)(2,1)} reshape(bf16[2,8,48,3,64]{4,3,2,1,0:T(4,128)(2,1)} %copy.42) | data formatting | bytes 589824 | tf_op jit(solution)/shard_map/reshape | solution.py:60
  90.0 20.9 %all_to_all.35 = bf16[16,48,192]{2,1,0:T(8,128)(2,1)S(1)} all-to-all(bf16[16,48,192]{2,1,0:T(8,128)(2,1)} %reshape.134), channel_id=1, replica_groups=mesh['tm'=48,'stripe'=16] {'stripe'}, dimensions={0} | all-to-all | bytes 589824 | tf_op jit(solution)/shard_map/all_to_all | solution.py:63
  110.9 0.5 fusion
  111.5 1.1 fusion.14
  112.6 1.7 %copy.47 = bf16[768,64]{1,0:T(8,128)(2,1)} copy(bf16[768,64]{0,1:T(8,128)(2,1)} %fusion.14) | data formatting | bytes 196608 | tf_op jit(solution)/shard_map/reshape | solution.py:75
  114.3 1.7 %reshape.148 = bf16[16,2,1536]{2,1,0:T(2,128)(2,1)} reshape(bf16[16,48,64]{2,1,0:T(8,128)(2,1)} %bitcast.82) | data formatting | bytes 196608
  116.0 12.8 %all_to_all.36 = bf16[16,2,1536]{2,1,0:T(2,128)(2,1)} all-to-all(bf16[16,2,1536]{2,1,0:T(2,128)(2,1)} %reshape.148), channel_id=1, replica_groups=mesh['tm'=48,'stripe'=16] {'stripe'}, dimensions={0} | all-to-all | bytes 196608 | tf_op jit(solution)/shard_map/all_to_all | solution.py:74
  128.8 1.8 %reshape.149 = bf16[16,48,64]{2,1,0:T(8,128)(2,1)} reshape(bf16[16,2,1536]{2,1,0:T(2,128)(2,1)} %all_to_all.36) | data formatting | bytes 196608
  130.6 1.6 %copy.50 = bf16[2,8,48,64]{3,1,2,0:T(8,128)(2,1)} copy(bf16[2,8,48,64]{3,2,1,0:T(8,128)(2,1)} %bitcast.83) | data formatting | bytes 196608 | tf_op jit(solution)/shard_map/reshape | solution.py:81
  132.2 1.7 %reshape.138 = bf16[96,512]{1,0:T(8,128)(2,1)} reshape(bf16[2,48,8,64]{3,2,1,0:T(8,128)(2,1)} %bitcast.84) | data formatting | bytes 196608 | tf_op jit(solution)/shard_map/reshape | solution.py:83
  134.0 2.3 %fusion.8 = bf16[96,1024]{1,0:T(8,128)(2,1)} fusion(f32[96,1024]{1,0:T(8,128)S(1)} %get-tuple-element.14, bf16[96,512]{1,0:T(8,128)(2,1)} %reshape.138, bf16[512,1024]{1,0:T(8,128)(2,1)} %param.9), kind=kOutput, calls=%fused_computation.11 | convolution fusion | flops 100859904 | bytes 1736704 | tf_op jit(solution)/shard_map/dot_general | solution.py:82
  (10 shorter events, 0.2 us)
Async XLA Ops:
  0.0 64.1 %copy-start = (bf16[1024,1536]{1,0:T(8,128)(2,1)S(1)}, bf16[1024,1536]{1,0:T(8,128)(2,1)}, u32[]{:S(2)}) copy-start(bf16[1024,1536]{1,0:T(8,128)(2,1)} %param.8) | copy-start | bytes 9437188
  2.0 33.2 %all-to-all-start = ((bf16[2,48,1024]{2,0,1:T(2,128)(2,1)}), bf16[2,48,1024]{2,0,1:T(2,128)(2,1)S(1)}, u32[]{:S(2)}, u32[]{:S(2)}) async-start(bf16[2,48,1024]{2,0,1:T(2,128)(2,1)} %copy.33), calls=%async_computation | async-start | bytes 393216 | tf_op jit(solution)/shard_map/all_to_all | solution.py:38

commit v2 on v1

v2 whole, which is shorter than its diff:
```python
import math

import jax
import jax.numpy as jnp
from jax import lax
from jax.experimental import pallas as pl
from jax.experimental.pallas import tpu as pltpu
from jax.sharding import PartitionSpec as P

HEAD_DIM = 64
LANES = 128
F32 = jnp.float32
BF16 = jnp.bfloat16
WEIGHT_SCALE = 2.0 / math.sqrt(HEAD_DIM) * math.log2(math.e)


def low_half(shape):
    return lax.broadcasted_iota(jnp.int32, shape, len(shape) - 1) < HEAD_DIM


def swap_halves(block):
    return pltpu.roll(block, HEAD_DIM, 1)


def layer_norm(wide):
    centre = jnp.mean(wide, axis=-1, keepdims=True)
    apart = wide - centre
    spread = jnp.mean(apart * apart, axis=-1, keepdims=True)
    return (apart * lax.rsqrt(spread + 1e-05)).astype(BF16)


def dot(left, right):
    return jnp.dot(left, right, preferred_element_type=F32)


def dot_t(left, right):
    return lax.dot_general(left, right, (((1,), (1,)), ((), ())), preferred_element_type=F32)


def packed_blocks(proj):
    rows, columns = proj.shape
    first = lax.broadcasted_iota(jnp.int32, (LANES, LANES), 0) // HEAD_DIM
    second = lax.broadcasted_iota(jnp.int32, (LANES, LANES), 1) // HEAD_DIM
    group = jnp.where(first == second, 1.0 / HEAD_DIM, 0.0).astype(BF16)
    low = low_half((rows, LANES))
    blocks = []
    for i in range(columns // LANES):
        block = proj[:, i * LANES : (i + 1) * LANES]
        square = block * block
        high = square.astype(BF16)
        rest = (square - high.astype(F32)).astype(BF16)
        factor = lax.rsqrt(dot(high, group) + dot(rest, group) + 1e-06)
        if i % 3 == 0:
            factor = jnp.where(low, factor * WEIGHT_SCALE, factor)
        elif i % 3 == 1:
            factor = jnp.where(low, 1.0, factor * WEIGHT_SCALE)
        else:
            factor = jnp.where(low, factor, 1.0)
        blocks.append(block * factor)
    return blocks


def send_tokens_kernel(tokens, out, rows):
    frames, patches, width = tokens.shape
    parts = width // LANES
    for f in range(frames):
        for c in range(parts):
            part = tokens[f, :, c * LANES : (c + 1) * LANES].astype(F32)
            rows[pl.ds(f * parts + c, patches, stride=frames * parts), :] = part
    out[...] = rows[...].reshape(out.shape).astype(BF16)


def time_kernel(tokens, weight, out, rows, sent):
    count, per, _ = tokens.shape
    width = weight.shape[0]
    parts = width // LANES
    span = count * per // parts
    rows[...] = tokens[...].astype(F32).reshape(rows.shape)
    wide = jnp.concatenate(
        [rows[pl.ds(c, span, stride=parts), :] for c in range(parts)], axis=1
    )
    blocks = packed_blocks(dot(layer_norm(wide), weight[...]))
    pairs = len(blocks) // 3
    low = low_half((span, LANES))
    for j in range(pairs):
        first, middle, last = blocks[3 * j : 3 * j + 3]
        mixed = jnp.where(low, last, middle)
        halves = []
        for query_key, is_low in ((first, True), (mixed, False)):
            keep = low if is_low else jnp.logical_not(low)
            query = jnp.where(keep, query_key, 0.0).astype(BF16)
            other = swap_halves(query_key).astype(BF16)
            weights = jnp.exp2(dot_t(query, other)).astype(BF16)
            value = jnp.where(keep, middle if is_low else last, 1.0).astype(BF16)
            halves.append(dot(weights, value))
        even, odd = halves
        total = swap_halves(jnp.where(low, odd, even))
        sent[pl.ds(j, span, stride=pairs), :] = jnp.where(low, even, odd) / total
    out[...] = sent[...].reshape(out.shape).astype(BF16)


def middle_kernel(attended, tokens, time_output, space_input, out, hidden_out, rows):
    frames, patches, width = tokens.shape
    inner = time_output.shape[0]
    parts = inner // LANES
    rows[...] = attended[...].astype(F32).reshape(rows.shape)
    back = jnp.concatenate(
        [
            jnp.concatenate(
                [
                    rows[pl.ds(f * parts + c, patches, stride=frames * parts), :]
                    for c in range(parts)
                ],
                axis=1,
            )
            for f in range(frames)
        ],
        axis=0,
    ).astype(BF16)
    wide = tokens[...].astype(F32).reshape(frames * patches, width)
    hidden = (wide + dot(back, time_output[...])).astype(BF16)
    hidden_out[...] = hidden
    blocks = packed_blocks(dot(layer_norm(hidden.astype(F32)), space_input[...]))
    pairs = len(blocks) // 3
    low = low_half((frames * patches, LANES))
    low_few = low_half((patches // 2, LANES))
    for j in range(pairs):
        first, middle, last = blocks[3 * j : 3 * j + 3]
        mixed = swap_halves(jnp.where(low, last, middle))
        for odd, query_key, value in ((0, first, middle), (1, mixed, last)):
            turned = swap_halves(value)
            lower, upper = (turned, value) if odd else (value, turned)
            for f in range(frames):
                start, half = f * patches, f * patches + patches // 2
                at = f * 2 * pairs + 2 * j + odd
                out[at, :patches, :] = query_key[start : start + patches].astype(BF16)
                out[at, patches:, :] = jnp.where(
                    low_few, lower[start:half], upper[half : start + patches]
                ).astype(BF16)


def space_kernel(pair, out):
    count, rows, _ = pair.shape
    half = rows // 3
    patches = 2 * half
    span = count * patches
    low = low_half((span, LANES))
    query_key = pair[:, :patches, :].reshape(span, LANES)
    wide = query_key.astype(F32)
    query = jnp.where(low, wide, 0.0).astype(BF16)
    keys = swap_halves(wide).astype(BF16)
    values = pair[:, patches:, :].astype(F32).reshape(count * half, LANES)
    turned = swap_halves(values)
    value = jnp.concatenate(
        [values.reshape(count, half, LANES), turned.reshape(count, half, LANES)], axis=1
    ).reshape(span, LANES)
    value = jnp.where(low, value, 1.0).astype(BF16)
    step = 4 * patches
    low_few = low_half((4, half, LANES))
    for i in range(span // step):
        weights = jnp.exp2(dot_t(query[i * step : (i + 1) * step], keys)).astype(BF16)
        summed = dot(weights, value)
        done = summed / swap_halves(summed)
        other = swap_halves(done).reshape(4, patches, LANES)
        done = done.reshape(4, patches, LANES)
        out[4 * i : 4 * i + 4] = jnp.where(low_few, done[:, :half], other[:, half:]).astype(BF16)


def final_kernel(back, hidden, weight, out):
    count, half, _ = back.shape
    frames, patches, width = out.shape
    heads = count // frames
    low = low_half((half, LANES))
    frame_rows = []
    for f in range(frames):
        columns = []
        for j in range(heads // 2):
            even = back[f * heads + 2 * j].astype(F32)
            odd = back[f * heads + 2 * j + 1].astype(F32)
            lower = jnp.where(low, even, swap_halves(odd))
            upper = jnp.where(low, swap_halves(even), odd)
            columns.append(jnp.concatenate([lower, upper], axis=0))
        frame_rows.append(jnp.concatenate(columns, axis=1))
    attended = jnp.concatenate(frame_rows, axis=0).astype(BF16)
    final = hidden[...].astype(F32) + dot(attended, weight[...])
    out[...] = final.astype(BF16).reshape(out.shape)


def call(kernel, out_shape, scratch, *args):
    return pl.pallas_call(
        kernel,
        out_shape=out_shape,
        in_specs=[pl.BlockSpec(memory_space=pltpu.VMEM)] * len(args),
        out_specs=jax.tree.map(lambda _: pl.BlockSpec(memory_space=pltpu.VMEM), out_shape),
        scratch_shapes=scratch,
    )(*args)


def array(*shape):
    return jax.ShapeDtypeStruct(shape, BF16)


def send_tokens(tokens):
    frames, patches, width = tokens.shape
    parts = width // LANES
    rows = pltpu.VMEM((frames * patches * parts, LANES), F32)
    return call(send_tokens_kernel, array(patches, frames * parts, LANES), [rows], tokens)


def time_half(moved, time_input):
    count, per, _ = moved.shape
    span = count * per * LANES // time_input.shape[0]
    parts = time_input.shape[1] // 3 // LANES
    rows = pltpu.VMEM((count * per, LANES), F32)
    sent = pltpu.VMEM((span * parts, LANES), F32)
    return call(
        time_kernel, array(count, span * parts // count, LANES), [rows, sent], moved, time_input
    )


def middle(returned, tokens, time_output, space_input):
    frames, patches, width = tokens.shape
    heads = time_output.shape[0] // HEAD_DIM
    count, per, _ = returned.shape
    rows = pltpu.VMEM((count * per, LANES), F32)
    shapes = (array(frames * heads, patches * 3 // 2, LANES), array(frames * patches, width))
    return call(middle_kernel, shapes, [rows], returned, tokens, time_output, space_input)


def space_half(pair):
    count, rows, _ = pair.shape
    return call(space_kernel, array(count, rows // 3, LANES), [], pair)


def final_half(back, hidden, space_output, shape):
    return call(final_kernel, array(*shape), [], back, hidden, space_output)


def per_device(tokens, time_input, time_output, space_input, space_output):
    moved = lax.all_to_all(send_tokens(tokens), "tm", 0, 0, tiled=True)
    attended = time_half(moved, time_input)
    returned = lax.all_to_all(attended, "tm", 0, 0, tiled=True)
    packed, hidden = middle(returned, tokens, time_output, space_input)
    pair = lax.all_to_all(packed, "stripe", 0, 0, tiled=True)
    back = lax.all_to_all(space_half(pair), "stripe", 0, 0, tiled=True)
    return final_half(back, hidden, space_output, tokens.shape)


def solution(mesh):
    placed = (P("tm", "stripe", None), P(), P(), P(), P())
    return jax.shard_map(
        per_device, mesh=mesh, in_specs=placed, out_specs=P("tm", "stripe", None), check_vma=False
    )
```

time: 137 us -> 103 us (0.75)
  blocking collectives: 54.2 us -> 86.1 us
  local copies, waits for them, and re-layouts: 28.2 us -> 0 us
  starting transfers between devices: 20 us -> 0 us
  Pallas kernels: 0 us -> 16.5 us
  other arithmetic: 14.8 us -> 0 us
  matrix products: 10.4 us -> 0 us
  waiting for transfers between devices: 8.52 us -> 0 us
    all_to_all x3 -> x4, blocking collectives: 54.2 us -> 86.1 us  [the longest x1 33.3 us: per_device(): moved = lax.all_to_all(send_tokens(tokens), 'tm', 0, 0, tiled=True)]
    all_to_all x1 -> x0, starting transfers between devices: 20 us -> none  [per_device(): lax.all_to_all(tokens, 'tm', split_axis=1, concat_axis=0, tiled=True)]
    pallas_call x0 -> x5, Pallas kernels: none -> 16.5 us  [call(): pl.pallas_call(kernel, out_shape=out_shape, in_specs=[pl.BlockSpec(memory...]
    reshape x6 -> x0, local copies, waits for them, and re-layouts: 10.7 us -> none  [the longest x1 2.77 us: per_device(): proj_space.reshape(frames, patches, heads, 3, HEAD_DIM)]
    dot_general x8 -> x0, matrix products: 10.4 us -> none  [the longest x1 2.86 us: per_device(): jnp.dot(layer_norm(moved), time_input, preferred_element_type=jnp.float32)]
    unnamed x9 -> x0, local copies, waits for them, and re-layouts: 10.3 us -> none
    all_to_all x1 -> x0, waiting for transfers between devices: 8.52 us -> none  [per_device(): lax.all_to_all(tokens, 'tm', split_axis=1, concat_axis=0, tiled=True)]
    reduce_sum x5 -> x0, other arithmetic: 6.67 us -> none  [the longest x2 5.85 us: normalize(): jnp.mean(query * query, axis=-1, keepdims=True) + 1e-06]
  transfers between devices with their start and end apart: 1 -> 0, of which waited for: 1 -> 0; matrix products, arithmetic and copies ran while one was open for 3% -> 0% of each run, Pallas kernels for 0% -> 0%
where the time goes in v2:
time: 103 us
  blocking collectives  86.1 us (84%)
  Pallas kernels  16.5 us (16%)
    all_to_all x1, blocking collectives, per_device(): moved = lax.all_to_all(send_tokens(tokens), 'tm', 0, 0, tiled=True)  33.3 us
    all_to_all x1, blocking collectives, per_device(): returned = lax.all_to_all(attended, 'tm', 0, 0, tiled=True)  20.1 us
    all_to_all x1, blocking collectives, per_device(): pair = lax.all_to_all(packed, 'stripe', 0, 0, tiled=True)  19.8 us
    pallas_call x5, Pallas kernels, call(): pl.pallas_call(kernel, out_shape=out_shape, in_specs=[pl.BlockSpec(memory...  16.5 us
    all_to_all x1, blocking collectives, per_device(): back = lax.all_to_all(space_half(pair), 'stripe', 0, 0, tiled=True)  12.8 us

profile of v2, /device:TPU:8, one launch (start us, length us, event | category | flops | bytes accessed | tf_op | source)
XLA Modules:
  0.0 102.6 jit_solution(2791264907802271235)
XLA Ops:
  0.0 1.8 %shard_map.55 = bf16[48,16,128]{2,1,0:T(8,128)(2,1)} custom-call(bf16[2,48,1024]{2,1,0:T(8,128)(2,1)} %tokens.3), custom_call_target="tpu_custom_call" | custom-call | tf_op jit(solution)/shard_map/pallas_call | solution.py:190
  1.8 33.3 %all_to_all.20.tokens = bf16[48,16,128]{2,1,0:T(8,128)(2,1)} all-to-all(bf16[48,16,128]{2,1,0:T(8,128)(2,1)} %shard_map.55), channel_id=1, replica_groups=mesh['tm'=48,'stripe'=16] {'tm'}, dimensions={0} | all-to-all | bytes 393216 | tf_op jit(solution)/shard_map/all_to_all | solution.py:240
  35.1 5.0 %shard_map.56 = bf16[48,8,128]{2,1,0:T(8,128)(2,1)} custom-call(bf16[48,16,128]{2,1,0:T(8,128)(2,1)} %all_to_all.20.tokens, bf16[1024,1536]{1,0:T(8,128)(2,1)} %weight.2), custom_call_target="tpu_custom_call" | custom-call | tf_op jit(solution)/shard_map/pallas_call | solution.py:190
  40.1 20.1 %all_to_all.21.attended = bf16[48,8,128]{2,1,0:T(8,128)(2,1)} all-to-all(bf16[48,8,128]{2,1,0:T(8,128)(2,1)} %shard_map.56), channel_id=1, replica_groups=mesh['tm'=48,'stripe'=16] {'tm'}, dimensions={0} | all-to-all | bytes 196608 | tf_op jit(solution)/shard_map/all_to_all | solution.py:242
  60.2 4.5 %shard_map.57 = (bf16[16,72,128]{2,1,0:T(8,128)(2,1)}, bf16[96,1024]{1,0:T(8,128)(2,1)}) custom-call(bf16[48,8,128]{2,1,0:T(8,128)(2,1)} %all_to_all.21.attended, bf16[2,48,1024]{2,1,0:T(8,128)(2,1)} %tokens.3, bf16[512,1024]{1,0:T(8,128)(2,1)} %time_output.1, bf16[1024,1536]{1,0:T(8,128)(2,1)} %space_input.1), custom_call_target="tpu_custom_call" | custom-call | tf_op jit(solution)/shard_map/pallas_call | solution.py:190
  64.7 19.8 %all_to_all.22.pair = bf16[16,72,128]{2,1,0:T(8,128)(2,1)} all-to-all(bf16[16,72,128]{2,1,0:T(8,128)(2,1)} %get-tuple-element.7), channel_id=1, replica_groups=mesh['tm'=48,'stripe'=16] {'stripe'}, dimensions={0} | all-to-all | bytes 589824 | tf_op jit(solution)/shard_map/all_to_all | solution.py:244
  84.5 2.8 %shard_map.58 = bf16[16,24,128]{2,1,0:T(8,128)(2,1)} custom-call(bf16[16,72,128]{2,1,0:T(8,128)(2,1)} %all_to_all.22.pair), custom_call_target="tpu_custom_call" | custom-call | tf_op jit(solution)/shard_map/pallas_call | solution.py:190
  87.3 12.8 %all_to_all.23.back = bf16[16,24,128]{2,1,0:T(8,128)(2,1)} all-to-all(bf16[16,24,128]{2,1,0:T(8,128)(2,1)} %shard_map.58), channel_id=1, replica_groups=mesh['tm'=48,'stripe'=16] {'stripe'}, dimensions={0} | all-to-all | bytes 196608 | tf_op jit(solution)/shard_map/all_to_all | solution.py:245
  100.2 2.4 %shard_map.59 = bf16[2,48,1024]{2,1,0:T(8,128)(2,1)} custom-call(bf16[16,24,128]{2,1,0:T(8,128)(2,1)} %all_to_all.23.back, bf16[96,1024]{1,0:T(8,128)(2,1)} %get-tuple-element.8.hidden, bf16[512,1024]{1,0:T(8,128)(2,1)} %weight.3), custom_call_target="tpu_custom_call" | custom-call | tf_op jit(solution)/shard_map/pallas_call | solution.py:190

commit v3 on v2

--- a/solution.py
+++ b/solution.py
@@ -12,6 +12,8 @@
 F32 = jnp.float32
 BF16 = jnp.bfloat16
 WEIGHT_SCALE = 2.0 / math.sqrt(HEAD_DIM) * math.log2(math.e)
+
+COST = pl.CostEstimate(flops=2 * 10**9, transcendentals=0, bytes_accessed=2 * 10**7)
 
 
 def low_half(shape):
@@ -186,25 +188,27 @@
     out[...] = final.astype(BF16).reshape(out.shape)
 
 
-def call(kernel, out_shape, scratch, *args):
+def call(kernel, out_shape, scratch, *args, cost=None):
     return pl.pallas_call(
         kernel,
         out_shape=out_shape,
         in_specs=[pl.BlockSpec(memory_space=pltpu.VMEM)] * len(args),
         out_specs=jax.tree.map(lambda _: pl.BlockSpec(memory_space=pltpu.VMEM), out_shape),
         scratch_shapes=scratch,
-    )(*args)
+        compiler_params=pltpu.CompilerParams(vmem_limit_bytes=12 * 2**20),
+        cost_estimate=cost,
+    )(*[pltpu.with_memory_space_constraint(arg, pltpu.VMEM) for arg in args])
 
 
 def array(*shape):
-    return jax.ShapeDtypeStruct(shape, BF16)
+    return pltpu.VMEM(shape, BF16)
 
 
 def send_tokens(tokens):
     frames, patches, width = tokens.shape
     parts = width // LANES
     rows = pltpu.VMEM((frames * patches * parts, LANES), F32)
-    return call(send_tokens_kernel, array(patches, frames * parts, LANES), [rows], tokens)
+    return call(send_tokens_kernel, array(patches, frames * parts, LANES), [rows], tokens, cost=COST)
 
 
 def time_half(moved, time_input):
@@ -233,7 +237,7 @@
 
 
 def final_half(back, hidden, space_output, shape):
-    return call(final_kernel, array(*shape), [], back, hidden, space_output)
+    return call(final_kernel, jax.ShapeDtypeStruct(shape, BF16), [], back, hidden, space_output)
 
 
 def per_device(tokens, time_input, time_output, space_input, space_output):

time: 103 us -> 92.6 us (0.90)
  Pallas kernels: 16.5 us -> 6.2 us
  local copies, waits for them, and re-layouts: 0 us -> 1.1 us
  blocking collectives: 86.1 us -> 85 us
    pallas_call x5, Pallas kernels: 16.5 us -> 6.2 us  [call(): pl.pallas_call(kernel, out_shape=out_shape, in_specs=[pl.BlockSpec(memory...]
    unnamed x0 -> x10, local copies, waits for them, and re-layouts: none -> 1.1 us
    all_to_all x1, blocking collectives: 19.8 us -> 18.8 us  [per_device(): pair = lax.all_to_all(packed, 'stripe', 0, 0, tiled=True)]
where the time goes in v3:
time: 92.6 us; the launch traced here: 92.4 us
  blocking collectives  85 us (92%)
  Pallas kernels  6.2 us (7%)
  local copies, waits for them, and re-layouts  1.1 us (1%)
    all_to_all x1, blocking collectives, per_device(): moved = lax.all_to_all(send_tokens(tokens), 'tm', 0, 0, tiled=True)  33.2 us
    all_to_all x1, blocking collectives, per_device(): returned = lax.all_to_all(attended, 'tm', 0, 0, tiled=True)  20.7 us
    all_to_all x1, blocking collectives, per_device(): pair = lax.all_to_all(packed, 'stripe', 0, 0, tiled=True)  18.8 us
    all_to_all x1, blocking collectives, per_device(): back = lax.all_to_all(space_half(pair), 'stripe', 0, 0, tiled=True)  12.4 us
    pallas_call x5, Pallas kernels, call(): pl.pallas_call(kernel, out_shape=out_shape, in_specs=[pl.BlockSpec(memory...  6.2 us

profile of v3, /device:TPU:8, one launch (start us, length us, event | category | flops | bytes accessed | tf_op | source)
XLA Modules:
  0.0 92.4 jit_solution(15497018096145863642)
XLA Ops:
  0.0 0.0 copy-start.1
  0.0 0.0 copy-start.4
  0.0 1.1 %copy-done.4 = bf16[2,48,1024]{2,1,0:T(8,128)(2,1)S(1)} copy-done((bf16[2,48,1024]{2,1,0:T(8,128)(2,1)S(1)}, bf16[2,48,1024]{2,1,0:T(8,128)(2,1)}, u32[]{:S(2)}) %copy-start.4) | copy-done | bytes 196632
  1.1 0.0 copy-start.2
  1.1 0.2 shard_map.55
  1.3 0.0 copy-start
  1.3 33.2 %all_to_all.20.tokens = bf16[48,16,128]{2,1,0:T(8,128)(2,1)S(1)} all-to-all(bf16[48,16,128]{2,1,0:T(8,128)(2,1)S(1)} %shard_map.55), channel_id=1, replica_groups=mesh['tm'=48,'stripe'=16] {'tm'}, dimensions={0} | all-to-all | bytes 393216 | tf_op jit(solution)/shard_map/all_to_all | solution.py:244
  34.5 0.0 copy-done.1
  34.5 2.3 %shard_map.56 = bf16[48,8,128]{2,1,0:T(8,128)(2,1)S(1)} custom-call(bf16[48,16,128]{2,1,0:T(8,128)(2,1)S(1)} %all_to_all.20.tokens, bf16[1024,1536]{1,0:T(8,128)(2,1)S(1)} %copy-done.1), custom_call_target="tpu_custom_call" | custom-call | tf_op jit(solution)/shard_map/pallas_call | solution.py:192
  36.9 0.0 copy-start.3
  36.9 20.7 %all_to_all.21.attended = bf16[48,8,128]{2,1,0:T(8,128)(2,1)S(1)} all-to-all(bf16[48,8,128]{2,1,0:T(8,128)(2,1)S(1)} %shard_map.56), channel_id=1, replica_groups=mesh['tm'=48,'stripe'=16] {'tm'}, dimensions={0} | all-to-all | bytes 196608 | tf_op jit(solution)/shard_map/all_to_all | solution.py:246
  57.6 0.0 copy-done.2
  57.6 0.0 copy-done
  57.6 1.4 %shard_map.57 = (bf16[16,72,128]{2,1,0:T(8,128)(2,1)S(1)}, bf16[96,1024]{1,0:T(8,128)(2,1)S(1)}) custom-call(bf16[48,8,128]{2,1,0:T(8,128)(2,1)S(1)} %all_to_all.21.attended, bf16[2,48,1024]{2,1,0:T(8,128)(2,1)S(1)} %copy-done.4, bf16[512,1024]{1,0:T(8,128)(2,1)S(1)} %copy-done.2, bf16[1024,1536]{1,0:T(8,128)(2,1)S(1)} %copy-done), custom_call_target="tpu_custom_call" | custom-call | tf_op jit(solution)/shard_map/pallas_call | solution.py:192
  59.0 18.8 %all_to_all.22.pair = bf16[16,72,128]{2,1,0:T(8,128)(2,1)S(1)} all-to-all(bf16[16,72,128]{2,1,0:T(8,128)(2,1)S(1)} %get-tuple-element.7), channel_id=1, replica_groups=mesh['tm'=48,'stripe'=16] {'stripe'}, dimensions={0} | all-to-all | bytes 589824 | tf_op jit(solution)/shard_map/all_to_all | solution.py:248
  77.7 1.2 %shard_map.58 = bf16[16,24,128]{2,1,0:T(8,128)(2,1)S(1)} custom-call(bf16[16,72,128]{2,1,0:T(8,128)(2,1)S(1)} %all_to_all.22.pair), custom_call_target="tpu_custom_call" | custom-call | tf_op jit(solution)/shard_map/pallas_call | solution.py:192
  79.0 12.4 %all_to_all.23.back = bf16[16,24,128]{2,1,0:T(8,128)(2,1)S(1)} all-to-all(bf16[16,24,128]{2,1,0:T(8,128)(2,1)S(1)} %shard_map.58), channel_id=1, replica_groups=mesh['tm'=48,'stripe'=16] {'stripe'}, dimensions={0} | all-to-all | bytes 196608 | tf_op jit(solution)/shard_map/all_to_all | solution.py:249
  91.3 0.0 copy-done.3
  91.3 1.0 %shard_map.59 = bf16[2,48,1024]{2,1,0:T(8,128)(2,1)} custom-call(bf16[16,24,128]{2,1,0:T(8,128)(2,1)S(1)} %all_to_all.23.back, bf16[96,1024]{1,0:T(8,128)(2,1)S(1)} %get-tuple-element.8.hidden, bf16[512,1024]{1,0:T(8,128)(2,1)S(1)} %copy-done.3), custom_call_target="tpu_custom_call" | custom-call | tf_op jit(solution)/shard_map/pallas_call | solution.py:192
Async XLA Ops:
  0.0 34.5 %copy-start.1 = (bf16[1024,1536]{1,0:T(8,128)(2,1)S(1)}, bf16[1024,1536]{1,0:T(8,128)(2,1)}, u32[]{:S(2)}) copy-start(bf16[1024,1536]{1,0:T(8,128)(2,1)} %weight.2) | copy-start | bytes 9437188
  0.0 1.1 %copy-start.4 = (bf16[2,48,1024]{2,1,0:T(8,128)(2,1)S(1)}, bf16[2,48,1024]{2,1,0:T(8,128)(2,1)}, u32[]{:S(2)}) copy-start(bf16[2,48,1024]{2,1,0:T(8,128)(2,1)} %tokens.3) | copy-start | bytes 589828
  1.1 56.5 %copy-start.2 = (bf16[512,1024]{1,0:T(8,128)(2,1)S(1)}, bf16[512,1024]{1,0:T(8,128)(2,1)}, u32[]{:S(2)}) copy-start(bf16[512,1024]{1,0:T(8,128)(2,1)} %time_output.1) | copy-start | bytes 3145732
  1.3 56.3 %copy-start = (bf16[1024,1536]{1,0:T(8,128)(2,1)S(1)}, bf16[1024,1536]{1,0:T(8,128)(2,1)}, u32[]{:S(2)}) copy-start(bf16[1024,1536]{1,0:T(8,128)(2,1)} %space_input.1) | copy-start | bytes 9437188
  36.9 54.5 %copy-start.3 = (bf16[512,1024]{1,0:T(8,128)(2,1)S(1)}, bf16[512,1024]{1,0:T(8,128)(2,1)}, u32[]{:S(2)}) copy-start(bf16[512,1024]{1,0:T(8,128)(2,1)} %weight.3) | copy-start | bytes 3145732

commit v4 on v3

--- a/solution.py
+++ b/solution.py
@@ -13,7 +13,7 @@
 BF16 = jnp.bfloat16
 WEIGHT_SCALE = 2.0 / math.sqrt(HEAD_DIM) * math.log2(math.e)
 
-COST = pl.CostEstimate(flops=2 * 10**9, transcendentals=0, bytes_accessed=2 * 10**7)
+AHEAD = pl.CostEstimate(flops=5 * 10**9, transcendentals=0, bytes_accessed=4 * 10**5)
 
 
 def low_half(shape):
@@ -41,24 +41,27 @@
 
 def packed_blocks(proj):
     rows, columns = proj.shape
-    first = lax.broadcasted_iota(jnp.int32, (LANES, LANES), 0) // HEAD_DIM
-    second = lax.broadcasted_iota(jnp.int32, (LANES, LANES), 1) // HEAD_DIM
+    first = lax.broadcasted_iota(jnp.int32, (2 * LANES, LANES), 0) // HEAD_DIM % 2
+    second = lax.broadcasted_iota(jnp.int32, (2 * LANES, LANES), 1) // HEAD_DIM
     group = jnp.where(first == second, 1.0 / HEAD_DIM, 0.0).astype(BF16)
     low = low_half((rows, LANES))
-    blocks = []
-    for i in range(columns // LANES):
-        block = proj[:, i * LANES : (i + 1) * LANES]
-        square = block * block
+    parts = [proj[:, i * LANES : (i + 1) * LANES] for i in range(columns // LANES)]
+    means = []
+    for part in parts:
+        square = part * part
         high = square.astype(BF16)
         rest = (square - high.astype(F32)).astype(BF16)
-        factor = lax.rsqrt(dot(high, group) + dot(rest, group) + 1e-06)
+        means.append(dot(jnp.concatenate([high, rest], axis=1), group))
+    blocks = []
+    for i, (part, mean) in enumerate(zip(parts, means, strict=True)):
+        factor = lax.rsqrt(mean + 1e-06)
         if i % 3 == 0:
             factor = jnp.where(low, factor * WEIGHT_SCALE, factor)
         elif i % 3 == 1:
             factor = jnp.where(low, 1.0, factor * WEIGHT_SCALE)
         else:
             factor = jnp.where(low, factor, 1.0)
-        blocks.append(block * factor)
+        blocks.append(part * factor)
     return blocks
 
 
@@ -84,18 +87,23 @@
     blocks = packed_blocks(dot(layer_norm(wide), weight[...]))
     pairs = len(blocks) // 3
     low = low_half((span, LANES))
+    high = jnp.logical_not(low)
+    heads = []
     for j in range(pairs):
         first, middle, last = blocks[3 * j : 3 * j + 3]
-        mixed = jnp.where(low, last, middle)
-        halves = []
-        for query_key, is_low in ((first, True), (mixed, False)):
-            keep = low if is_low else jnp.logical_not(low)
-            query = jnp.where(keep, query_key, 0.0).astype(BF16)
-            other = swap_halves(query_key).astype(BF16)
-            weights = jnp.exp2(dot_t(query, other)).astype(BF16)
-            value = jnp.where(keep, middle if is_low else last, 1.0).astype(BF16)
-            halves.append(dot(weights, value))
-        even, odd = halves
+        heads.append((low, first, middle))
+        heads.append((high, jnp.where(low, last, middle), last))
+    scores = [
+        dot_t(jnp.where(keep, both, 0.0).astype(BF16), swap_halves(both).astype(BF16))
+        for keep, both, _ in heads
+    ]
+    weights = [jnp.exp2(score).astype(BF16) for score in scores]
+    summed = [
+        dot(weight, jnp.where(keep, block, 1.0).astype(BF16))
+        for weight, (keep, _, block) in zip(weights, heads, strict=True)
+    ]
+    for j in range(pairs):
+        even, odd = summed[2 * j : 2 * j + 2]
         total = swap_halves(jnp.where(low, odd, even))
         sent[pl.ds(j, span, stride=pairs), :] = jnp.where(low, even, odd) / total
     out[...] = sent[...].reshape(out.shape).astype(BF16)
@@ -157,15 +165,13 @@
         [values.reshape(count, half, LANES), turned.reshape(count, half, LANES)], axis=1
     ).reshape(span, LANES)
     value = jnp.where(low, value, 1.0).astype(BF16)
-    step = 4 * patches
-    low_few = low_half((4, half, LANES))
-    for i in range(span // step):
-        weights = jnp.exp2(dot_t(query[i * step : (i + 1) * step], keys)).astype(BF16)
-        summed = dot(weights, value)
-        done = summed / swap_halves(summed)
-        other = swap_halves(done).reshape(4, patches, LANES)
-        done = done.reshape(4, patches, LANES)
-        out[4 * i : 4 * i + 4] = jnp.where(low_few, done[:, :half], other[:, half:]).astype(BF16)
+    weights = jnp.exp2(dot_t(query, keys)).astype(BF16)
+    summed = dot(weights, value)
+    done = summed / swap_halves(summed)
+    other = swap_halves(done).reshape(count, patches, LANES)
+    done = done.reshape(count, patches, LANES)
+    low_few = low_half((count, half, LANES))
+    out[...] = jnp.where(low_few, done[:, :half], other[:, half:]).astype(BF16)
 
 
 def final_kernel(back, hidden, weight, out):
@@ -208,7 +214,7 @@
     frames, patches, width = tokens.shape
     parts = width // LANES
     rows = pltpu.VMEM((frames * patches * parts, LANES), F32)
-    return call(send_tokens_kernel, array(patches, frames * parts, LANES), [rows], tokens, cost=COST)
+    return call(send_tokens_kernel, array(patches, frames * parts, LANES), [rows], tokens, cost=AHEAD)
 
 
 def time_half(moved, time_input):
@@ -217,9 +223,8 @@
     parts = time_input.shape[1] // 3 // LANES
     rows = pltpu.VMEM((count * per, LANES), F32)
     sent = pltpu.VMEM((span * parts, LANES), F32)
-    return call(
-        time_kernel, array(count, span * parts // count, LANES), [rows, sent], moved, time_input
-    )
+    shape = array(count, span * parts // count, LANES)
+    return call(time_kernel, shape, [rows, sent], moved, time_input, cost=AHEAD)
 
 
 def middle(returned, tokens, time_output, space_input):

time: 92.6 us -> 91.3 us (0.986)
  Pallas kernels: 6.2 us -> 5.12 us
    pallas_call x5, Pallas kernels: 6.2 us -> 5.12 us  [call(): pl.pallas_call(kernel, out_shape=out_shape, in_specs=[pl.BlockSpec(memory...]
where the time goes in v4:
time: 91.3 us; the launch traced here: 91 us
  blocking collectives  84.9 us (93%)
  Pallas kernels  5.12 us (6%)
  local copies, waits for them, and re-layouts  0.95 us (1%)
    all_to_all x1, blocking collectives, per_device(): moved = lax.all_to_all(send_tokens(tokens), 'tm', 0, 0, tiled=True)  33.1 us
    all_to_all x1, blocking collectives, per_device(): returned = lax.all_to_all(attended, 'tm', 0, 0, tiled=True)  20.7 us
    all_to_all x1, blocking collectives, per_device(): pair = lax.all_to_all(packed, 'stripe', 0, 0, tiled=True)  18.8 us
    all_to_all x1, blocking collectives, per_device(): back = lax.all_to_all(space_half(pair), 'stripe', 0, 0, tiled=True)  12.4 us
    pallas_call x5, Pallas kernels, call(): pl.pallas_call(kernel, out_shape=out_shape, in_specs=[pl.BlockSpec(memory...  5.12 us

profile of v4, /device:TPU:8, one launch (start us, length us, event | category | flops | bytes accessed | tf_op | source)
XLA Modules:
  0.0 91.0 jit_solution(16492157703472667029)
XLA Ops:
  0.0 0.0 copy-start.3
  0.0 0.9 %copy-done.3 = bf16[2,48,1024]{2,1,0:T(8,128)(2,1)S(1)} copy-done((bf16[2,48,1024]{2,1,0:T(8,128)(2,1)S(1)}, bf16[2,48,1024]{2,1,0:T(8,128)(2,1)}, u32[]{:S(2)}) %copy-start.3) | copy-done | bytes 196632
  0.9 0.0 copy-start.5
  0.9 0.2 shard_map.55
  1.1 33.1 %all_to_all.20.tokens = bf16[48,16,128]{2,1,0:T(8,128)(2,1)S(1)} all-to-all(bf16[48,16,128]{2,1,0:T(8,128)(2,1)S(1)} %shard_map.55), channel_id=1, replica_groups=mesh['tm'=48,'stripe'=16] {'tm'}, dimensions={0} | all-to-all | bytes 393216 | tf_op jit(solution)/shard_map/all_to_all | solution.py:249
  34.2 0.0 copy-done.5
  34.2 0.0 copy-start
  34.2 0.0 copy-start.1
  34.2 0.0 copy-start.4
  34.3 1.5 %shard_map.56 = bf16[48,8,128]{2,1,0:T(8,128)(2,1)S(1)} custom-call(bf16[48,16,128]{2,1,0:T(8,128)(2,1)S(1)} %all_to_all.20.tokens, bf16[1024,1536]{1,0:T(8,128)(2,1)S(1)} %copy-done.5), custom_call_target="tpu_custom_call" | custom-call | flops 5000000000 | bytes 400000 | tf_op jit(solution)/shard_map/pallas_call | solution.py:198
  35.7 0.0 copy-start.2
  35.7 20.7 %all_to_all.21.attended = bf16[48,8,128]{2,1,0:T(8,128)(2,1)S(1)} all-to-all(bf16[48,8,128]{2,1,0:T(8,128)(2,1)S(1)} %shard_map.56), channel_id=1, replica_groups=mesh['tm'=48,'stripe'=16] {'tm'}, dimensions={0} | all-to-all | bytes 196608 | tf_op jit(solution)/shard_map/all_to_all | solution.py:251
  56.4 0.0 copy-done
  56.4 0.0 copy-done.1
  56.4 0.0 copy-done.4
  56.4 1.3 %shard_map.57 = (bf16[16,72,128]{2,1,0:T(8,128)(2,1)S(1)}, bf16[96,1024]{1,0:T(8,128)(2,1)S(1)}) custom-call(bf16[48,8,128]{2,1,0:T(8,128)(2,1)S(1)} %all_to_all.21.attended, bf16[2,48,1024]{2,1,0:T(8,128)(2,1)S(1)} %copy-done.4, bf16[512,1024]{1,0:T(8,128)(2,1)S(1)} %copy-done.1, bf16[1024,1536]{1,0:T(8,128)(2,1)S(1)} %copy-done), custom_call_target="tpu_custom_call" | custom-call | tf_op jit(solution)/shard_map/pallas_call | solution.py:198
  57.7 18.8 %all_to_all.22.pair = bf16[16,72,128]{2,1,0:T(8,128)(2,1)S(1)} all-to-all(bf16[16,72,128]{2,1,0:T(8,128)(2,1)S(1)} %get-tuple-element.7), channel_id=1, replica_groups=mesh['tm'=48,'stripe'=16] {'stripe'}, dimensions={0} | all-to-all | bytes 589824 | tf_op jit(solution)/shard_map/all_to_all | solution.py:253
  76.5 1.1 %shard_map.58 = bf16[16,24,128]{2,1,0:T(8,128)(2,1)S(1)} custom-call(bf16[16,72,128]{2,1,0:T(8,128)(2,1)S(1)} %all_to_all.22.pair), custom_call_target="tpu_custom_call" | custom-call | tf_op jit(solution)/shard_map/pallas_call | solution.py:198
  77.6 12.4 %all_to_all.23.back = bf16[16,24,128]{2,1,0:T(8,128)(2,1)S(1)} all-to-all(bf16[16,24,128]{2,1,0:T(8,128)(2,1)S(1)} %shard_map.58), channel_id=1, replica_groups=mesh['tm'=48,'stripe'=16] {'stripe'}, dimensions={0} | all-to-all | bytes 196608 | tf_op jit(solution)/shard_map/all_to_all | solution.py:254
  90.0 0.0 copy-done.2
  90.0 1.0 %shard_map.59 = bf16[2,48,1024]{2,1,0:T(8,128)(2,1)} custom-call(bf16[16,24,128]{2,1,0:T(8,128)(2,1)S(1)} %all_to_all.23.back, bf16[96,1024]{1,0:T(8,128)(2,1)S(1)} %get-tuple-element.8.hidden, bf16[512,1024]{1,0:T(8,128)(2,1)S(1)} %copy-done.2), custom_call_target="tpu_custom_call" | custom-call | tf_op jit(solution)/shard_map/pallas_call | solution.py:198
Async XLA Ops:
  0.0 0.9 %copy-start.3 = (bf16[2,48,1024]{2,1,0:T(8,128)(2,1)S(1)}, bf16[2,48,1024]{2,1,0:T(8,128)(2,1)}, u32[]{:S(2)}) copy-start(bf16[2,48,1024]{2,1,0:T(8,128)(2,1)} %tokens.3) | copy-start | bytes 589828
  0.9 33.3 %copy-start.5 = (bf16[1024,1536]{1,0:T(8,128)(2,1)S(1)}, bf16[1024,1536]{1,0:T(8,128)(2,1)}, u32[]{:S(2)}) copy-start(bf16[1024,1536]{1,0:T(8,128)(2,1)} %weight.2) | copy-start | bytes 9437188
  34.2 22.1 %copy-start = (bf16[1024,1536]{1,0:T(8,128)(2,1)S(1)}, bf16[1024,1536]{1,0:T(8,128)(2,1)}, u32[]{:S(2)}) copy-start(bf16[1024,1536]{1,0:T(8,128)(2,1)} %space_input.1) | copy-start | bytes 9437188
  34.2 22.1 %copy-start.1 = (bf16[512,1024]{1,0:T(8,128)(2,1)S(1)}, bf16[512,1024]{1,0:T(8,128)(2,1)}, u32[]{:S(2)}) copy-start(bf16[512,1024]{1,0:T(8,128)(2,1)} %time_output.1) | copy-start | bytes 3145732
  34.2 22.1 %copy-start.4 = (bf16[2,48,1024]{2,1,0:T(8,128)(2,1)S(1)}, bf16[2,48,1024]{2,1,0:T(8,128)(2,1)}, u32[]{:S(2)}) copy-start(bf16[2,48,1024]{2,1,0:T(8,128)(2,1)} %tokens.3) | copy-start | bytes 589828
  35.7 54.3 %copy-start.2 = (bf16[512,1024]{1,0:T(8,128)(2,1)S(1)}, bf16[512,1024]{1,0:T(8,128)(2,1)}, u32[]{:S(2)}) copy-start(bf16[512,1024]{1,0:T(8,128)(2,1)} %weight.3) | copy-start | bytes 3145732

commit v5 on v4

--- a/solution.py
+++ b/solution.py
@@ -13,6 +13,7 @@
 BF16 = jnp.bfloat16
 WEIGHT_SCALE = 2.0 / math.sqrt(HEAD_DIM) * math.log2(math.e)
 
+TIME_FIRST = 28
 AHEAD = pl.CostEstimate(flops=5 * 10**9, transcendentals=0, bytes_accessed=4 * 10**5)
 
 
@@ -165,8 +166,10 @@
         [values.reshape(count, half, LANES), turned.reshape(count, half, LANES)], axis=1
     ).reshape(span, LANES)
     value = jnp.where(low, value, 1.0).astype(BF16)
-    weights = jnp.exp2(dot_t(query, keys)).astype(BF16)
-    summed = dot(weights, value)
+    half_span = span // 2
+    scores = [dot_t(query[i : i + half_span], keys) for i in (0, half_span)]
+    weights = [jnp.exp2(score).astype(BF16) for score in scores]
+    summed = jnp.concatenate([dot(weight, value) for weight in weights], axis=0)
     done = summed / swap_halves(summed)
     other = swap_halves(done).reshape(count, patches, LANES)
     done = done.reshape(count, patches, LANES)
@@ -245,13 +248,20 @@
     return call(final_kernel, jax.ShapeDtypeStruct(shape, BF16), [], back, hidden, space_output)
 
 
+def exchange(messages, axis, order):
+    return lax.all_to_all(messages, axis, 0, 0, tiled=True, axis_index_groups=[order])
+
+
 def per_device(tokens, time_input, time_output, space_input, space_output):
-    moved = lax.all_to_all(send_tokens(tokens), "tm", 0, 0, tiled=True)
+    time_count = lax.axis_size("tm")
+    time_order = [(TIME_FIRST + i) % time_count for i in range(time_count)]
+    stripe_order = list(reversed(range(lax.axis_size("stripe"))))
+    moved = exchange(send_tokens(tokens), "tm", time_order)
     attended = time_half(moved, time_input)
-    returned = lax.all_to_all(attended, "tm", 0, 0, tiled=True)
+    returned = exchange(attended, "tm", time_order)
     packed, hidden = middle(returned, tokens, time_output, space_input)
-    pair = lax.all_to_all(packed, "stripe", 0, 0, tiled=True)
-    back = lax.all_to_all(space_half(pair), "stripe", 0, 0, tiled=True)
+    pair = exchange(packed, "stripe", stripe_order)
+    back = exchange(space_half(pair), "stripe", stripe_order)
     return final_half(back, hidden, space_output, tokens.shape)
 
 

time: 91.3 us -> 82.2 us (0.900)
  blocking collectives: 84.9 us -> 75.9 us
    all_to_all x4, blocking collectives: 84.9 us -> 75.9 us  [exchange(): lax.all_to_all(messages, axis, 0, 0, tiled=True, axis_index_groups=[order])]
where the time goes in v5:
time: 82.2 us; the launch traced here: 81.9 us
  blocking collectives  75.9 us (92%)
  Pallas kernels  5.01 us (6%)
  local copies, waits for them, and re-layouts  0.95 us (1%)
    all_to_all x4, blocking collectives, exchange(): lax.all_to_all(messages, axis, 0, 0, tiled=True, axis_index_groups=[order])  75.9 us
    pallas_call x5, Pallas kernels, call(): pl.pallas_call(kernel, out_shape=out_shape, in_specs=[pl.BlockSpec(memory...  5.01 us

profile of v5, /device:TPU:8, one launch (start us, length us, event | category | flops | bytes accessed | tf_op | source)
XLA Modules:
  0.0 81.9 jit_solution(5574741253823486674)
XLA Ops:
  0.0 0.0 copy-start.3
  0.0 0.9 %copy-done.3 = bf16[2,48,1024]{2,1,0:T(8,128)(2,1)S(1)} copy-done((bf16[2,48,1024]{2,1,0:T(8,128)(2,1)S(1)}, bf16[2,48,1024]{2,1,0:T(8,128)(2,1)}, u32[]{:S(2)}) %copy-start.3) | copy-done | bytes 196632
  0.9 0.0 copy-start.5
  0.9 0.2 shard_map.55
  1.1 30.5 %all_to_all.20.tokens = bf16[48,16,128]{2,1,0:T(8,128)(2,1)S(1)} all-to-all(bf16[48,16,128]{2,1,0:T(8,128)(2,1)S(1)} %shard_map.55), channel_id=1, replica_groups={{448,464,480,496,512,528,544,560,576,592,608,624,640,656,672,688,704,72..., dimensions={0} | all-to-all | bytes 393216 | tf_op jit(solution)/shard_map/all_to_all | solution.py:252
  31.6 0.0 copy-done.5
  31.6 0.0 copy-start
  31.6 0.0 copy-start.1
  31.6 0.0 copy-start.4
  31.6 1.5 %shard_map.56 = bf16[48,8,128]{2,1,0:T(8,128)(2,1)S(1)} custom-call(bf16[48,16,128]{2,1,0:T(8,128)(2,1)S(1)} %all_to_all.20.tokens, bf16[1024,1536]{1,0:T(8,128)(2,1)S(1)} %copy-done.5), custom_call_target="tpu_custom_call" | custom-call | flops 5000000000 | bytes 400000 | tf_op jit(solution)/shard_map/pallas_call | solution.py:201
  33.1 0.0 copy-start.2
  33.1 18.7 %all_to_all.21.attended = bf16[48,8,128]{2,1,0:T(8,128)(2,1)S(1)} all-to-all(bf16[48,8,128]{2,1,0:T(8,128)(2,1)S(1)} %shard_map.56), channel_id=1, replica_groups={{448,464,480,496,512,528,544,560,576,592,608,624,640,656,672,688,704,72..., dimensions={0} | all-to-all | bytes 196608 | tf_op jit(solution)/shard_map/all_to_all | solution.py:252
  51.8 0.0 copy-done
  51.8 0.0 copy-done.1
  51.8 0.0 copy-done.4
  51.8 1.3 %shard_map.57 = (bf16[16,72,128]{2,1,0:T(8,128)(2,1)S(1)}, bf16[96,1024]{1,0:T(8,128)(2,1)S(1)}) custom-call(bf16[48,8,128]{2,1,0:T(8,128)(2,1)S(1)} %all_to_all.21.attended, bf16[2,48,1024]{2,1,0:T(8,128)(2,1)S(1)} %copy-done.4, bf16[512,1024]{1,0:T(8,128)(2,1)S(1)} %copy-done.1, bf16[1024,1536]{1,0:T(8,128)(2,1)S(1)} %copy-done), custom_call_target="tpu_custom_call" | custom-call | tf_op jit(solution)/shard_map/pallas_call | solution.py:201
  53.2 15.4 %all_to_all.22.pair = bf16[16,72,128]{2,1,0:T(8,128)(2,1)S(1)} all-to-all(bf16[16,72,128]{2,1,0:T(8,128)(2,1)S(1)} %get-tuple-element.7), channel_id=1, replica_groups={{15,14,13,12,11,10,9,8,7,6,5,4,3,2,1,0},{31,30,29,28,27,26,25,24,23,22,..., dimensions={0} | all-to-all | bytes 589824 | tf_op jit(solution)/shard_map/all_to_all | solution.py:252
  68.6 1.0 %shard_map.58 = bf16[16,24,128]{2,1,0:T(8,128)(2,1)S(1)} custom-call(bf16[16,72,128]{2,1,0:T(8,128)(2,1)S(1)} %all_to_all.22.pair), custom_call_target="tpu_custom_call" | custom-call | tf_op jit(solution)/shard_map/pallas_call | solution.py:201
  69.6 11.4 %all_to_all.23.back = bf16[16,24,128]{2,1,0:T(8,128)(2,1)S(1)} all-to-all(bf16[16,24,128]{2,1,0:T(8,128)(2,1)S(1)} %shard_map.58), channel_id=1, replica_groups={{15,14,13,12,11,10,9,8,7,6,5,4,3,2,1,0},{31,30,29,28,27,26,25,24,23,22,..., dimensions={0} | all-to-all | bytes 196608 | tf_op jit(solution)/shard_map/all_to_all | solution.py:252
  80.9 0.0 copy-done.2
  80.9 1.0 %shard_map.59 = bf16[2,48,1024]{2,1,0:T(8,128)(2,1)} custom-call(bf16[16,24,128]{2,1,0:T(8,128)(2,1)S(1)} %all_to_all.23.back, bf16[96,1024]{1,0:T(8,128)(2,1)S(1)} %get-tuple-element.8.hidden, bf16[512,1024]{1,0:T(8,128)(2,1)S(1)} %copy-done.2), custom_call_target="tpu_custom_call" | custom-call | tf_op jit(solution)/shard_map/pallas_call | solution.py:201
Async XLA Ops:
  0.0 0.9 %copy-start.3 = (bf16[2,48,1024]{2,1,0:T(8,128)(2,1)S(1)}, bf16[2,48,1024]{2,1,0:T(8,128)(2,1)}, u32[]{:S(2)}) copy-start(bf16[2,48,1024]{2,1,0:T(8,128)(2,1)} %tokens.3) | copy-start | bytes 589828
  0.9 30.7 %copy-start.5 = (bf16[1024,1536]{1,0:T(8,128)(2,1)S(1)}, bf16[1024,1536]{1,0:T(8,128)(2,1)}, u32[]{:S(2)}) copy-start(bf16[1024,1536]{1,0:T(8,128)(2,1)} %weight.2) | copy-start | bytes 9437188
  31.6 20.2 %copy-start = (bf16[1024,1536]{1,0:T(8,128)(2,1)S(1)}, bf16[1024,1536]{1,0:T(8,128)(2,1)}, u32[]{:S(2)}) copy-start(bf16[1024,1536]{1,0:T(8,128)(2,1)} %space_input.1) | copy-start | bytes 9437188
  31.6 20.2 %copy-start.1 = (bf16[512,1024]{1,0:T(8,128)(2,1)S(1)}, bf16[512,1024]{1,0:T(8,128)(2,1)}, u32[]{:S(2)}) copy-start(bf16[512,1024]{1,0:T(8,128)(2,1)} %time_output.1) | copy-start | bytes 3145732
  31.6 20.2 %copy-start.4 = (bf16[2,48,1024]{2,1,0:T(8,128)(2,1)S(1)}, bf16[2,48,1024]{2,1,0:T(8,128)(2,1)}, u32[]{:S(2)}) copy-start(bf16[2,48,1024]{2,1,0:T(8,128)(2,1)} %tokens.3) | copy-start | bytes 589828
  33.1 47.8 %copy-start.2 = (bf16[512,1024]{1,0:T(8,128)(2,1)S(1)}, bf16[512,1024]{1,0:T(8,128)(2,1)}, u32[]{:S(2)}) copy-start(bf16[512,1024]{1,0:T(8,128)(2,1)} %weight.3) | copy-start | bytes 3145732

commit v6 on v5

--- a/solution.py
+++ b/solution.py
@@ -13,7 +13,8 @@
 BF16 = jnp.bfloat16
 WEIGHT_SCALE = 2.0 / math.sqrt(HEAD_DIM) * math.log2(math.e)
 
-TIME_FIRST = 28
+TIME_FIRST = 29
+STRIPE_FIRST = 10
 AHEAD = pl.CostEstimate(flops=5 * 10**9, transcendentals=0, bytes_accessed=4 * 10**5)
 
 
@@ -255,7 +256,8 @@
 def per_device(tokens, time_input, time_output, space_input, space_output):
     time_count = lax.axis_size("tm")
     time_order = [(TIME_FIRST + i) % time_count for i in range(time_count)]
-    stripe_order = list(reversed(range(lax.axis_size("stripe"))))
+    others = [i for i in range(lax.axis_size("stripe")) if i != STRIPE_FIRST]
+    stripe_order = [STRIPE_FIRST, *others]
     moved = exchange(send_tokens(tokens), "tm", time_order)
     attended = time_half(moved, time_input)
     returned = exchange(attended, "tm", time_order)

time: 82.2 us -> 79.6 us (0.968)
  blocking collectives: 75.9 us -> 73.4 us
    all_to_all x4, blocking collectives: 75.9 us -> 73.4 us  [exchange(): lax.all_to_all(messages, axis, 0, 0, tiled=True, axis_index_groups=[order])]
where the time goes in v6:
time: 79.6 us; the launch traced here: 79.4 us
  blocking collectives  73.4 us (92%)
  Pallas kernels  5.01 us (6%)
  local copies, waits for them, and re-layouts  0.95 us (1%)
    all_to_all x4, blocking collectives, exchange(): lax.all_to_all(messages, axis, 0, 0, tiled=True, axis_index_groups=[order])  73.4 us
    pallas_call x5, Pallas kernels, call(): pl.pallas_call(kernel, out_shape=out_shape, in_specs=[pl.BlockSpec(memory...  5.01 us

profile of v6, /device:TPU:8, one launch (start us, length us, event | category | flops | bytes accessed | tf_op | source)
XLA Modules:
  0.0 79.4 jit_solution(498950146080576018)
XLA Ops:
  0.0 0.0 copy-start.3
  0.0 0.9 %copy-done.3 = bf16[2,48,1024]{2,1,0:T(8,128)(2,1)S(1)} copy-done((bf16[2,48,1024]{2,1,0:T(8,128)(2,1)S(1)}, bf16[2,48,1024]{2,1,0:T(8,128)(2,1)}, u32[]{:S(2)}) %copy-start.3) | copy-done | bytes 196632
  0.9 0.0 copy-start.5
  0.9 0.2 shard_map.55
  1.1 30.2 %all_to_all.20.tokens = bf16[48,16,128]{2,1,0:T(8,128)(2,1)S(1)} all-to-all(bf16[48,16,128]{2,1,0:T(8,128)(2,1)S(1)} %shard_map.55), channel_id=1, replica_groups={{464,480,496,512,528,544,560,576,592,608,624,640,656,672,688,704,720,73..., dimensions={0} | all-to-all | bytes 393216 | tf_op jit(solution)/shard_map/all_to_all | solution.py:253
  31.3 0.0 copy-done.5
  31.3 0.0 copy-start
  31.4 0.0 copy-start.1
  31.4 0.0 copy-start.4
  31.4 1.5 %shard_map.56 = bf16[48,8,128]{2,1,0:T(8,128)(2,1)S(1)} custom-call(bf16[48,16,128]{2,1,0:T(8,128)(2,1)S(1)} %all_to_all.20.tokens, bf16[1024,1536]{1,0:T(8,128)(2,1)S(1)} %copy-done.5), custom_call_target="tpu_custom_call" | custom-call | flops 5000000000 | bytes 400000 | tf_op jit(solution)/shard_map/pallas_call | solution.py:202
  32.8 0.0 copy-start.2
  32.8 18.2 %all_to_all.21.attended = bf16[48,8,128]{2,1,0:T(8,128)(2,1)S(1)} all-to-all(bf16[48,8,128]{2,1,0:T(8,128)(2,1)S(1)} %shard_map.56), channel_id=1, replica_groups={{464,480,496,512,528,544,560,576,592,608,624,640,656,672,688,704,720,73..., dimensions={0} | all-to-all | bytes 196608 | tf_op jit(solution)/shard_map/all_to_all | solution.py:253
  51.0 0.0 copy-done
  51.0 0.0 copy-done.1
  51.1 0.0 copy-done.4
  51.1 1.3 %shard_map.57 = (bf16[16,72,128]{2,1,0:T(8,128)(2,1)S(1)}, bf16[96,1024]{1,0:T(8,128)(2,1)S(1)}) custom-call(bf16[48,8,128]{2,1,0:T(8,128)(2,1)S(1)} %all_to_all.21.attended, bf16[2,48,1024]{2,1,0:T(8,128)(2,1)S(1)} %copy-done.4, bf16[512,1024]{1,0:T(8,128)(2,1)S(1)} %copy-done.1, bf16[1024,1536]{1,0:T(8,128)(2,1)S(1)} %copy-done), custom_call_target="tpu_custom_call" | custom-call | tf_op jit(solution)/shard_map/pallas_call | solution.py:202
  52.4 13.7 %all_to_all.22.pair = bf16[16,72,128]{2,1,0:T(8,128)(2,1)S(1)} all-to-all(bf16[16,72,128]{2,1,0:T(8,128)(2,1)S(1)} %get-tuple-element.7), channel_id=1, replica_groups={{10,0,1,2,3,4,5,6,7,8,9,11,12,13,14,15},{26,16,17,18,19,20,21,22,23,24,..., dimensions={0} | all-to-all | bytes 589824 | tf_op jit(solution)/shard_map/all_to_all | solution.py:253
  66.1 1.0 %shard_map.58 = bf16[16,24,128]{2,1,0:T(8,128)(2,1)S(1)} custom-call(bf16[16,72,128]{2,1,0:T(8,128)(2,1)S(1)} %all_to_all.22.pair), custom_call_target="tpu_custom_call" | custom-call | tf_op jit(solution)/shard_map/pallas_call | solution.py:202
  67.1 11.3 %all_to_all.23.back = bf16[16,24,128]{2,1,0:T(8,128)(2,1)S(1)} all-to-all(bf16[16,24,128]{2,1,0:T(8,128)(2,1)S(1)} %shard_map.58), channel_id=1, replica_groups={{10,0,1,2,3,4,5,6,7,8,9,11,12,13,14,15},{26,16,17,18,19,20,21,22,23,24,..., dimensions={0} | all-to-all | bytes 196608 | tf_op jit(solution)/shard_map/all_to_all | solution.py:253
  78.4 0.0 copy-done.2
  78.4 1.0 %shard_map.59 = bf16[2,48,1024]{2,1,0:T(8,128)(2,1)} custom-call(bf16[16,24,128]{2,1,0:T(8,128)(2,1)S(1)} %all_to_all.23.back, bf16[96,1024]{1,0:T(8,128)(2,1)S(1)} %get-tuple-element.8.hidden, bf16[512,1024]{1,0:T(8,128)(2,1)S(1)} %copy-done.2), custom_call_target="tpu_custom_call" | custom-call | tf_op jit(solution)/shard_map/pallas_call | solution.py:202
Async XLA Ops:
  0.0 0.9 %copy-start.3 = (bf16[2,48,1024]{2,1,0:T(8,128)(2,1)S(1)}, bf16[2,48,1024]{2,1,0:T(8,128)(2,1)}, u32[]{:S(2)}) copy-start(bf16[2,48,1024]{2,1,0:T(8,128)(2,1)} %tokens.3) | copy-start | bytes 589828
  0.9 30.4 %copy-start.5 = (bf16[1024,1536]{1,0:T(8,128)(2,1)S(1)}, bf16[1024,1536]{1,0:T(8,128)(2,1)}, u32[]{:S(2)}) copy-start(bf16[1024,1536]{1,0:T(8,128)(2,1)} %weight.2) | copy-start | bytes 9437188
  31.3 19.7 %copy-start = (bf16[1024,1536]{1,0:T(8,128)(2,1)S(1)}, bf16[1024,1536]{1,0:T(8,128)(2,1)}, u32[]{:S(2)}) copy-start(bf16[1024,1536]{1,0:T(8,128)(2,1)} %space_input.1) | copy-start | bytes 9437188
  31.4 19.7 %copy-start.1 = (bf16[512,1024]{1,0:T(8,128)(2,1)S(1)}, bf16[512,1024]{1,0:T(8,128)(2,1)}, u32[]{:S(2)}) copy-start(bf16[512,1024]{1,0:T(8,128)(2,1)} %time_output.1) | copy-start | bytes 3145732
  31.4 19.7 %copy-start.4 = (bf16[2,48,1024]{2,1,0:T(8,128)(2,1)S(1)}, bf16[2,48,1024]{2,1,0:T(8,128)(2,1)}, u32[]{:S(2)}) copy-start(bf16[2,48,1024]{2,1,0:T(8,128)(2,1)} %tokens.3) | copy-start | bytes 589828
  32.8 45.5 %copy-start.2 = (bf16[512,1024]{1,0:T(8,128)(2,1)S(1)}, bf16[512,1024]{1,0:T(8,128)(2,1)}, u32[]{:S(2)}) copy-start(bf16[512,1024]{1,0:T(8,128)(2,1)} %weight.3) | copy-start | bytes 3145732

commit v7 on v6

--- a/solution.py
+++ b/solution.py
@@ -175,7 +175,14 @@
     other = swap_halves(done).reshape(count, patches, LANES)
     done = done.reshape(count, patches, LANES)
     low_few = low_half((count, half, LANES))
-    out[...] = jnp.where(low_few, done[:, :half], other[:, half:]).astype(BF16)
+    messages = jnp.where(low_few, done[:, :half], other[:, half:]).astype(BF16)
+    out[...] = messages
+    out[0] = messages[STRIPE_FIRST]
+    out[STRIPE_FIRST] = messages[0]
+
+
+def traded(place):
+    return {0: STRIPE_FIRST, STRIPE_FIRST: 0}.get(place, place)
 
 
 def final_kernel(back, hidden, weight, out):
@@ -187,8 +194,8 @@
     for f in range(frames):
         columns = []
         for j in range(heads // 2):
-            even = back[f * heads + 2 * j].astype(F32)
-            odd = back[f * heads + 2 * j + 1].astype(F32)
+            even = back[traded(f * heads + 2 * j)].astype(F32)
+            odd = back[traded(f * heads + 2 * j + 1)].astype(F32)
             lower = jnp.where(low, even, swap_halves(odd))
             upper = jnp.where(low, swap_halves(even), odd)
             columns.append(jnp.concatenate([lower, upper], axis=0))
@@ -256,14 +263,16 @@
 def per_device(tokens, time_input, time_output, space_input, space_output):
     time_count = lax.axis_size("tm")
     time_order = [(TIME_FIRST + i) % time_count for i in range(time_count)]
-    others = [i for i in range(lax.axis_size("stripe")) if i != STRIPE_FIRST]
-    stripe_order = [STRIPE_FIRST, *others]
+    stripe_order, back_order = (
+        [first, *(i for i in range(lax.axis_size("stripe")) if i != first)]
+        for first in (STRIPE_FIRST, STRIPE_FIRST - 1)
+    )
     moved = exchange(send_tokens(tokens), "tm", time_order)
     attended = time_half(moved, time_input)
     returned = exchange(attended, "tm", time_order)
     packed, hidden = middle(returned, tokens, time_output, space_input)
     pair = exchange(packed, "stripe", stripe_order)
-    back = exchange(space_half(pair), "stripe", stripe_order)
+    back = exchange(space_half(pair), "stripe", back_order)
     return final_half(back, hidden, space_output, tokens.shape)
 
 

time: 79.6 us -> 81.1 us (1.019)
  blocking collectives: 73.4 us -> 74.9 us
    all_to_all x4, blocking collectives: 73.4 us -> 74.9 us  [exchange(): lax.all_to_all(messages, axis, 0, 0, tiled=True, axis_index_groups=[order])]
where the time goes in v7:
time: 81.1 us; the launch traced here: 80.9 us
  blocking collectives  74.9 us (92%)
  Pallas kernels  5.01 us (6%)
  local copies, waits for them, and re-layouts  0.95 us (1%)
    all_to_all x4, blocking collectives, exchange(): lax.all_to_all(messages, axis, 0, 0, tiled=True, axis_index_groups=[order])  74.9 us
    pallas_call x5, Pallas kernels, call(): pl.pallas_call(kernel, out_shape=out_shape, in_specs=[pl.BlockSpec(memory...  5.01 us

profile of v7, /device:TPU:8, one launch (start us, length us, event | category | flops | bytes accessed | tf_op | source)
XLA Modules:
  0.0 80.9 jit_solution(15304975349022124887)
XLA Ops:
  0.0 0.0 copy-start.3
  0.0 0.9 %copy-done.3 = bf16[2,48,1024]{2,1,0:T(8,128)(2,1)S(1)} copy-done((bf16[2,48,1024]{2,1,0:T(8,128)(2,1)S(1)}, bf16[2,48,1024]{2,1,0:T(8,128)(2,1)}, u32[]{:S(2)}) %copy-start.3) | copy-done | bytes 196632
  0.9 0.0 copy-start.5
  0.9 0.2 shard_map.55
  1.1 30.2 %all_to_all.20.tokens = bf16[48,16,128]{2,1,0:T(8,128)(2,1)S(1)} all-to-all(bf16[48,16,128]{2,1,0:T(8,128)(2,1)S(1)} %shard_map.55), channel_id=1, replica_groups={{464,480,496,512,528,544,560,576,592,608,624,640,656,672,688,704,720,73..., dimensions={0} | all-to-all | bytes 393216 | tf_op jit(solution)/shard_map/all_to_all | solution.py:260
  31.3 0.0 copy-done.5
  31.3 0.0 copy-start
  31.4 0.0 copy-start.1
  31.4 0.0 copy-start.4
  31.4 1.5 %shard_map.56 = bf16[48,8,128]{2,1,0:T(8,128)(2,1)S(1)} custom-call(bf16[48,16,128]{2,1,0:T(8,128)(2,1)S(1)} %all_to_all.20.tokens, bf16[1024,1536]{1,0:T(8,128)(2,1)S(1)} %copy-done.5), custom_call_target="tpu_custom_call" | custom-call | flops 5000000000 | bytes 400000 | tf_op jit(solution)/shard_map/pallas_call | solution.py:209
  32.8 0.0 copy-start.2
  32.8 18.2 %all_to_all.21.attended = bf16[48,8,128]{2,1,0:T(8,128)(2,1)S(1)} all-to-all(bf16[48,8,128]{2,1,0:T(8,128)(2,1)S(1)} %shard_map.56), channel_id=1, replica_groups={{464,480,496,512,528,544,560,576,592,608,624,640,656,672,688,704,720,73..., dimensions={0} | all-to-all | bytes 196608 | tf_op jit(solution)/shard_map/all_to_all | solution.py:260
  51.0 0.0 copy-done
  51.0 0.0 copy-done.1
  51.1 0.0 copy-done.4
  51.1 1.3 %shard_map.57 = (bf16[16,72,128]{2,1,0:T(8,128)(2,1)S(1)}, bf16[96,1024]{1,0:T(8,128)(2,1)S(1)}) custom-call(bf16[48,8,128]{2,1,0:T(8,128)(2,1)S(1)} %all_to_all.21.attended, bf16[2,48,1024]{2,1,0:T(8,128)(2,1)S(1)} %copy-done.4, bf16[512,1024]{1,0:T(8,128)(2,1)S(1)} %copy-done.1, bf16[1024,1536]{1,0:T(8,128)(2,1)S(1)} %copy-done), custom_call_target="tpu_custom_call" | custom-call | tf_op jit(solution)/shard_map/pallas_call | solution.py:209
  52.4 13.7 %all_to_all.22.pair = bf16[16,72,128]{2,1,0:T(8,128)(2,1)S(1)} all-to-all(bf16[16,72,128]{2,1,0:T(8,128)(2,1)S(1)} %get-tuple-element.7), channel_id=1, replica_groups={{10,0,1,2,3,4,5,6,7,8,9,11,12,13,14,15},{26,16,17,18,19,20,21,22,23,24,..., dimensions={0} | all-to-all | bytes 589824 | tf_op jit(solution)/shard_map/all_to_all | solution.py:260
  66.1 1.0 %shard_map.58 = bf16[16,24,128]{2,1,0:T(8,128)(2,1)S(1)} custom-call(bf16[16,72,128]{2,1,0:T(8,128)(2,1)S(1)} %all_to_all.22.pair), custom_call_target="tpu_custom_call" | custom-call | tf_op jit(solution)/shard_map/pallas_call | solution.py:209
  67.1 12.8 %all_to_all.23.back = bf16[16,24,128]{2,1,0:T(8,128)(2,1)S(1)} all-to-all(bf16[16,24,128]{2,1,0:T(8,128)(2,1)S(1)} %shard_map.58), channel_id=1, replica_groups={{9,0,1,2,3,4,5,6,7,8,10,11,12,13,14,15},{25,16,17,18,19,20,21,22,23,24,..., dimensions={0} | all-to-all | bytes 196608 | tf_op jit(solution)/shard_map/all_to_all | solution.py:260
  79.9 0.0 copy-done.2
  79.9 1.0 %shard_map.59 = bf16[2,48,1024]{2,1,0:T(8,128)(2,1)} custom-call(bf16[16,24,128]{2,1,0:T(8,128)(2,1)S(1)} %all_to_all.23.back, bf16[96,1024]{1,0:T(8,128)(2,1)S(1)} %get-tuple-element.8.hidden, bf16[512,1024]{1,0:T(8,128)(2,1)S(1)} %copy-done.2), custom_call_target="tpu_custom_call" | custom-call | tf_op jit(solution)/shard_map/pallas_call | solution.py:209
Async XLA Ops:
  0.0 0.9 %copy-start.3 = (bf16[2,48,1024]{2,1,0:T(8,128)(2,1)S(1)}, bf16[2,48,1024]{2,1,0:T(8,128)(2,1)}, u32[]{:S(2)}) copy-start(bf16[2,48,1024]{2,1,0:T(8,128)(2,1)} %tokens.3) | copy-start | bytes 589828
  0.9 30.4 %copy-start.5 = (bf16[1024,1536]{1,0:T(8,128)(2,1)S(1)}, bf16[1024,1536]{1,0:T(8,128)(2,1)}, u32[]{:S(2)}) copy-start(bf16[1024,1536]{1,0:T(8,128)(2,1)} %weight.2) | copy-start | bytes 9437188
  31.3 19.7 %copy-start = (bf16[1024,1536]{1,0:T(8,128)(2,1)S(1)}, bf16[1024,1536]{1,0:T(8,128)(2,1)}, u32[]{:S(2)}) copy-start(bf16[1024,1536]{1,0:T(8,128)(2,1)} %space_input.1) | copy-start | bytes 9437188
  31.4 19.7 %copy-start.1 = (bf16[512,1024]{1,0:T(8,128)(2,1)S(1)}, bf16[512,1024]{1,0:T(8,128)(2,1)}, u32[]{:S(2)}) copy-start(bf16[512,1024]{1,0:T(8,128)(2,1)} %time_output.1) | copy-start | bytes 3145732
  31.4 19.7 %copy-start.4 = (bf16[2,48,1024]{2,1,0:T(8,128)(2,1)S(1)}, bf16[2,48,1024]{2,1,0:T(8,128)(2,1)}, u32[]{:S(2)}) copy-start(bf16[2,48,1024]{2,1,0:T(8,128)(2,1)} %tokens.3) | copy-start | bytes 589828
  32.8 47.0 %copy-start.2 = (bf16[512,1024]{1,0:T(8,128)(2,1)S(1)}, bf16[512,1024]{1,0:T(8,128)(2,1)}, u32[]{:S(2)}) copy-start(bf16[512,1024]{1,0:T(8,128)(2,1)} %weight.3) | copy-start | bytes 3145732

commit v8 on v7

--- a/solution.py
+++ b/solution.py
@@ -15,6 +15,7 @@
 
 TIME_FIRST = 29
 STRIPE_FIRST = 10
+BACK_FIRST = 14
 AHEAD = pl.CostEstimate(flops=5 * 10**9, transcendentals=0, bytes_accessed=4 * 10**5)
 
 
@@ -177,12 +178,12 @@
     low_few = low_half((count, half, LANES))
     messages = jnp.where(low_few, done[:, :half], other[:, half:]).astype(BF16)
     out[...] = messages
-    out[0] = messages[STRIPE_FIRST]
-    out[STRIPE_FIRST] = messages[0]
+    out[0] = messages[BACK_FIRST]
+    out[BACK_FIRST] = messages[0]
 
 
 def traded(place):
-    return {0: STRIPE_FIRST, STRIPE_FIRST: 0}.get(place, place)
+    return {0: BACK_FIRST, BACK_FIRST: 0}.get(place, place)
 
 
 def final_kernel(back, hidden, weight, out):
@@ -263,10 +264,9 @@
 def per_device(tokens, time_input, time_output, space_input, space_output):
     time_count = lax.axis_size("tm")
     time_order = [(TIME_FIRST + i) % time_count for i in range(time_count)]
-    stripe_order, back_order = (
-        [first, *(i for i in range(lax.axis_size("stripe")) if i != first)]
-        for first in (STRIPE_FIRST, STRIPE_FIRST - 1)
-    )
+    others = [i for i in range(lax.axis_size("stripe")) if i != STRIPE_FIRST]
+    stripe_order = [STRIPE_FIRST, *others]
+    back_order = [stripe_order[traded(i)] for i in range(len(stripe_order))]
     moved = exchange(send_tokens(tokens), "tm", time_order)
     attended = time_half(moved, time_input)
     returned = exchange(attended, "tm", time_order)

time: 81.1 us -> 80 us (0.986)
  the two profiles are of different devices: /device:TPU:8 before, /device:TPU:6 now
where the time goes in v8:
time: 80 us; the launch traced here: 79.7 us
  blocking collectives  73.7 us (92%)
  Pallas kernels  5.02 us (6%)
  local copies, waits for them, and re-layouts  0.95 us (1%)
    all_to_all x4, blocking collectives, exchange(): lax.all_to_all(messages, axis, 0, 0, tiled=True, axis_index_groups=[order])  73.7 us
    pallas_call x5, Pallas kernels, call(): pl.pallas_call(kernel, out_shape=out_shape, in_specs=[pl.BlockSpec(memory...  5.02 us

profile of v8, /device:TPU:6, one launch (start us, length us, event | category | flops | bytes accessed | tf_op | source)
XLA Modules:
  0.0 79.7 jit_solution(15195402432002286879)
XLA Ops:
  0.0 0.0 copy-start.3
  0.0 0.9 %copy-done.3 = bf16[2,48,1024]{2,1,0:T(8,128)(2,1)S(1)} copy-done((bf16[2,48,1024]{2,1,0:T(8,128)(2,1)S(1)}, bf16[2,48,1024]{2,1,0:T(8,128)(2,1)}, u32[]{:S(2)}) %copy-start.3) | copy-done | bytes 196632
  0.9 0.0 copy-start.5
  0.9 0.2 shard_map.55
  1.1 30.3 %all_to_all.20.tokens = bf16[48,16,128]{2,1,0:T(8,128)(2,1)S(1)} all-to-all(bf16[48,16,128]{2,1,0:T(8,128)(2,1)S(1)} %shard_map.55), channel_id=1, replica_groups={{464,480,496,512,528,544,560,576,592,608,624,640,656,672,688,704,720,73..., dimensions={0} | all-to-all | bytes 393216 | tf_op jit(solution)/shard_map/all_to_all | solution.py:261
  31.4 0.0 copy-done.5
  31.4 0.0 copy-start
  31.5 0.0 copy-start.1
  31.5 0.0 copy-start.4
  31.5 1.5 %shard_map.56 = bf16[48,8,128]{2,1,0:T(8,128)(2,1)S(1)} custom-call(bf16[48,16,128]{2,1,0:T(8,128)(2,1)S(1)} %all_to_all.20.tokens, bf16[1024,1536]{1,0:T(8,128)(2,1)S(1)} %copy-done.5), custom_call_target="tpu_custom_call" | custom-call | flops 5000000000 | bytes 400000 | tf_op jit(solution)/shard_map/pallas_call | solution.py:210
  32.9 0.0 copy-start.2
  32.9 18.2 %all_to_all.21.attended = bf16[48,8,128]{2,1,0:T(8,128)(2,1)S(1)} all-to-all(bf16[48,8,128]{2,1,0:T(8,128)(2,1)S(1)} %shard_map.56), channel_id=1, replica_groups={{464,480,496,512,528,544,560,576,592,608,624,640,656,672,688,704,720,73..., dimensions={0} | all-to-all | bytes 196608 | tf_op jit(solution)/shard_map/all_to_all | solution.py:261
  51.1 0.0 copy-done
  51.1 0.0 copy-done.1
  51.1 0.0 copy-done.4
  51.2 1.3 %shard_map.57 = (bf16[16,72,128]{2,1,0:T(8,128)(2,1)S(1)}, bf16[96,1024]{1,0:T(8,128)(2,1)S(1)}) custom-call(bf16[48,8,128]{2,1,0:T(8,128)(2,1)S(1)} %all_to_all.21.attended, bf16[2,48,1024]{2,1,0:T(8,128)(2,1)S(1)} %copy-done.4, bf16[512,1024]{1,0:T(8,128)(2,1)S(1)} %copy-done.1, bf16[1024,1536]{1,0:T(8,128)(2,1)S(1)} %copy-done), custom_call_target="tpu_custom_call" | custom-call | tf_op jit(solution)/shard_map/pallas_call | solution.py:210
  52.5 14.0 %all_to_all.22.pair = bf16[16,72,128]{2,1,0:T(8,128)(2,1)S(1)} all-to-all(bf16[16,72,128]{2,1,0:T(8,128)(2,1)S(1)} %get-tuple-element.7), channel_id=1, replica_groups={{10,0,1,2,3,4,5,6,7,8,9,11,12,13,14,15},{26,16,17,18,19,20,21,22,23,24,..., dimensions={0} | all-to-all | bytes 589824 | tf_op jit(solution)/shard_map/all_to_all | solution.py:261
  66.5 1.0 %shard_map.58 = bf16[16,24,128]{2,1,0:T(8,128)(2,1)S(1)} custom-call(bf16[16,72,128]{2,1,0:T(8,128)(2,1)S(1)} %all_to_all.22.pair), custom_call_target="tpu_custom_call" | custom-call | tf_op jit(solution)/shard_map/pallas_call | solution.py:210
  67.5 11.1 %all_to_all.23.back = bf16[16,24,128]{2,1,0:T(8,128)(2,1)S(1)} all-to-all(bf16[16,24,128]{2,1,0:T(8,128)(2,1)S(1)} %shard_map.58), channel_id=1, replica_groups={{14,0,1,2,3,4,5,6,7,8,9,11,12,13,10,15},{30,16,17,18,19,20,21,22,23,24,..., dimensions={0} | all-to-all | bytes 196608 | tf_op jit(solution)/shard_map/all_to_all | solution.py:261
  78.7 0.0 copy-done.2
  78.7 1.0 %shard_map.59 = bf16[2,48,1024]{2,1,0:T(8,128)(2,1)} custom-call(bf16[16,24,128]{2,1,0:T(8,128)(2,1)S(1)} %all_to_all.23.back, bf16[96,1024]{1,0:T(8,128)(2,1)S(1)} %get-tuple-element.8.hidden, bf16[512,1024]{1,0:T(8,128)(2,1)S(1)} %copy-done.2), custom_call_target="tpu_custom_call" | custom-call | tf_op jit(solution)/shard_map/pallas_call | solution.py:210
Async XLA Ops:
  0.0 0.9 %copy-start.3 = (bf16[2,48,1024]{2,1,0:T(8,128)(2,1)S(1)}, bf16[2,48,1024]{2,1,0:T(8,128)(2,1)}, u32[]{:S(2)}) copy-start(bf16[2,48,1024]{2,1,0:T(8,128)(2,1)} %tokens.3) | copy-start | bytes 589828
  0.9 30.5 %copy-start.5 = (bf16[1024,1536]{1,0:T(8,128)(2,1)S(1)}, bf16[1024,1536]{1,0:T(8,128)(2,1)}, u32[]{:S(2)}) copy-start(bf16[1024,1536]{1,0:T(8,128)(2,1)} %weight.2) | copy-start | bytes 9437188
  31.4 19.7 %copy-start = (bf16[1024,1536]{1,0:T(8,128)(2,1)S(1)}, bf16[1024,1536]{1,0:T(8,128)(2,1)}, u32[]{:S(2)}) copy-start(bf16[1024,1536]{1,0:T(8,128)(2,1)} %space_input.1) | copy-start | bytes 9437188
  31.5 19.7 %copy-start.1 = (bf16[512,1024]{1,0:T(8,128)(2,1)S(1)}, bf16[512,1024]{1,0:T(8,128)(2,1)}, u32[]{:S(2)}) copy-start(bf16[512,1024]{1,0:T(8,128)(2,1)} %time_output.1) | copy-start | bytes 3145732
  31.5 19.7 %copy-start.4 = (bf16[2,48,1024]{2,1,0:T(8,128)(2,1)S(1)}, bf16[2,48,1024]{2,1,0:T(8,128)(2,1)}, u32[]{:S(2)}) copy-start(bf16[2,48,1024]{2,1,0:T(8,128)(2,1)} %tokens.3) | copy-start | bytes 589828
  32.9 45.8 %copy-start.2 = (bf16[512,1024]{1,0:T(8,128)(2,1)S(1)}, bf16[512,1024]{1,0:T(8,128)(2,1)}, u32[]{:S(2)}) copy-start(bf16[512,1024]{1,0:T(8,128)(2,1)} %weight.3) | copy-start | bytes 3145732
